TPU v7x, 256 devices: a whole 4x4x8 slice. The times are simulated.
256 devices in a mesh: seq: 8 (over z), chan: 16 (over y, x), rep: 2 (over core).
Axes of the slice: x: 4, y: 4, z: 8, core: 2. Of those that a mesh axis runs over, the one named last changes fastest.
Arguments:
- fine_codes: int32 [16384], P(('rep', 'seq')), parts along dimension 0, may hold values from 0 to 1023
- coarse_codes: int32 [8192], P(('rep', 'seq')), parts along dimension 0, may hold values from 0 to 1023
- frame_order: int32 [256], replicated, may hold values from 0 to 255, each once
- emb_fine: bfloat16 [1024, 4096], P(None, 'chan'), may hold values from -90 to 90
- emb_coarse: bfloat16 [1024, 4096], P(None, 'chan'), may hold values from -90 to 90
- norm_gain: bfloat16 [4096], P('chan'), may hold values from 0.099609375 to 1.8984375
- w_hyena: bfloat16 [4096, 3, 4096], P(None, None, 'chan'), may hold values from -0.09375 to 0.09375
- short_taps: bfloat16 [3, 256, 128], P(None, 'chan'), may hold values from -0.5 to 0.5
- long_filter: float32 [4096, 8192], P(('chan', 'seq')), may hold values from -5 to 5
- w_attn: bfloat16 [4096, 3, 2048], P(None, None, 'chan'), may hold values from -0.09375 to 0.09375
Outputs:
- hyena_out: bfloat16 [4096, 16384], P('chan', ('rep', 'seq')), parts along dimension 1
- attn_out: bfloat16 [16384, 2048], P(('rep', 'seq'), 'chan'), parts along dimension 0
There are 2 independent parts, one for each index of `rep`. A program takes and returns all parts, laid end to end along the dimension named above; an argument that names none is the same for every part. Nothing has to cross between parts.
Inputs may be any that keep to these rules, and one draw needn't show every extreme that they name: `frame_order`: each of 0 to 255 once.
All inputs are finite; a program needn't handle non-finite values.
Results may differ from a plain program's by a relative error of at most 0.014.
The roundings to bfloat16 on the way count: a program that leaves them out, or rounds other values in their place, can miss the bound.
Values may be sent and summed in bfloat16 or wider, within the bound.
A program may use at most 128 MiB of HBM per device.

v0:
```python
import functools
import math

import jax
import jax.numpy as jnp
import numpy as np
from jax import lax
from jax.experimental import pallas as pl
from jax.experimental.pallas import tpu as pltpu
from jax.sharding import PartitionSpec as P

HD = 128
FRAME = 256
BLOCK = 512
LANES = 128
EPSILON = 1e-05
F32 = jnp.float32
BF16 = jnp.bfloat16
ANY = pl.BlockSpec(memory_space=pl.ANY)
MESH = pl.DeviceIdType.MESH
BIG = 56 << 20

ROWS_W = 72
TILES = 64
POINTS = 2 * TILES * LANES


def split_np(x):
    hi = np.asarray(x, np.float32).astype(jnp.bfloat16)
    lo = (np.asarray(x, np.float64) - hi.astype(np.float64)).astype(np.float32).astype(jnp.bfloat16)
    return hi, lo


@functools.lru_cache(None)
def tables():
    w = np.arange(ROWS_W)[:, None]
    kept = (w <= 64).astype(np.float64)
    q = np.arange(TILES)[None, :]
    angle = 2 * np.pi * ((w * q) % 128) / 128
    outer = np.concatenate([np.cos(angle) * kept, -np.sin(angle) * kept], 0)
    a = np.arange(LANES)[None, :]
    turn = 2 * np.pi * (w * a) / POINTS
    twist = np.stack([np.cos(turn) * kept, np.sin(turn) * kept]).astype(np.float32)
    m = np.arange(LANES)
    inner = 2 * np.pi * ((m[:, None] * m[None, :]) % 128) / 128
    c, s = np.cos(inner), np.sin(inner)
    forward = np.block([[c, -s], [s, c]])
    backward = np.block([[c, s], [-s, c]])
    weight = np.where((w == 0) | (w == 64), 1.0, 2.0) * kept / POINTS
    inverse = np.concatenate([(np.cos(angle) * weight).T, (-np.sin(angle) * weight).T], 1)
    outer_hi, outer_lo = split_np(outer)
    inv_hi, inv_lo = split_np(inverse)
    fwd = np.stack(split_np(forward))
    bwd = np.stack(split_np(backward))
    outer3 = np.concatenate([outer_hi, outer_lo, outer_hi], 1)
    inv3 = np.concatenate([inv_hi, inv_lo, inv_hi], 1)
    return outer3, twist, fwd, bwd, inv3


def split(x):
    hi = x.astype(BF16)
    return hi, (x - hi.astype(F32)).astype(BF16)


def mm(a, b):
    return jnp.dot(a, b, preferred_element_type=F32)


def mm3(x, table):
    hi, lo = split(x)
    return mm(hi, table[0]) + (mm(lo, table[0]) + mm(hi, table[1]))


def ids_kernel(fine_ref, coarse_ref, order_ref, emb_fine_ref, emb_coarse_ref, ids_ref, sums_ref):
    order = order_ref[...]
    row = lax.broadcasted_iota(jnp.int32, (FRAME, FRAME), 0)
    pick = (row == order).astype(BF16)
    pick_half = (row[: FRAME // 2] == order // 2).astype(BF16)

    def looked(codes, pick):
        hi = (codes // 32).astype(F32).astype(BF16)
        lo = (codes % 32).astype(F32).astype(BF16)
        return (mm(hi, pick) * 32.0 + mm(lo, pick)).astype(jnp.int32)

    fine = looked(fine_ref[...], pick)
    coarse = looked(coarse_ref[...], pick_half)
    ids_ref[0:4, :] = fine
    ids_ref[4:8, :] = coarse
    vocab = lax.broadcasted_iota(jnp.int32, (emb_fine_ref.shape[0], FRAME), 0)
    dims = (((0,), (0,)), ((), ()))
    for frame in range(4):
        hot_fine = (vocab == fine[frame : frame + 1]).astype(BF16)
        hot_coarse = (vocab == coarse[frame : frame + 1]).astype(BF16)
        rows = lax.dot_general(emb_fine_ref[...], hot_fine, dims, preferred_element_type=F32)
        rows = rows + lax.dot_general(
            emb_coarse_ref[...], hot_coarse, dims, preferred_element_type=F32
        )
        rows = rows.astype(BF16).astype(F32)
        total = jnp.sum(rows * rows, axis=0, keepdims=True)
        sums_ref[2 * frame : 2 * frame + 1, :] = total[:, :LANES]
        sums_ref[2 * frame + 1 : 2 * frame + 2, :] = total[:, LANES:]


def local_ids(fine, coarse, order, emb_fine, emb_coarse, interpret=False):
    return pl.pallas_call(
        ids_kernel,
        out_shape=(
            jax.ShapeDtypeStruct((8, FRAME), jnp.int32),
            jax.ShapeDtypeStruct((8, LANES), F32),
        ),
        compiler_params=pltpu.CompilerParams(vmem_limit_bytes=BIG),
        interpret=interpret,
        name="local_ids",
    )(fine.reshape(4, FRAME), coarse.reshape(4, FRAME // 2), order[None], emb_fine, emb_coarse)


def project_kernel(rows_ref, side_ref, w_ref, out_ref, factor_ref, x_ref):
    chans = rows_ref.shape[0]

    @pl.when(pl.program_id(0) == 0)
    def _():
        for c in range(chans):
            x = rows_ref[c].astype(F32) * side_ref[c, 0:1, :FRAME]
            hi, lo = split(x)
            x_ref[0:128, c * 256 : (c + 1) * 256] = hi
            x_ref[128:256, c * 256 : (c + 1) * 256] = lo
        total = side_ref[0, :, FRAME:]
        for c in range(1, chans):
            total = total + side_ref[c, :, FRAME:]
        factor_ref[...] = lax.rsqrt(total / (chans * 256.0) + EPSILON)

    both = mm(x_ref[...], w_ref[0])
    hi, lo = split(jnp.transpose(both[:128] + both[128:]))
    out_ref[0, :, :128] = hi
    out_ref[0, :, 128:] = lo


def project(rows, side, w, interpret=False):
    chans = rows.shape[0]
    depth = w.shape[1]
    return pl.pallas_call(
        project_kernel,
        grid=(3,),
        in_specs=[
            pl.BlockSpec(rows.shape, lambda k: (0, 0, 0)),
            pl.BlockSpec(side.shape, lambda k: (0, 0, 0)),
            pl.BlockSpec((1, depth, 256), lambda k: (k, 0, 0)),
        ],
        out_specs=[
            pl.BlockSpec((1, 256, 256), lambda k: (k, 0, 0)),
            pl.BlockSpec((8, LANES), lambda k: (0, 0)),
        ],
        out_shape=(
            jax.ShapeDtypeStruct((3, 256, 256), BF16),
            jax.ShapeDtypeStruct((8, LANES), F32),
        ),
        scratch_shapes=[pltpu.VMEM((256, chans * 256), BF16)],
        compiler_params=pltpu.CompilerParams(vmem_limit_bytes=BIG),
        interpret=interpret,
        name="project",
    )(rows, side, w)


GROUP = 4


def twisted(step, twist_ref):
    cos, sin = twist_ref[0], twist_ref[1]
    rows = []
    for i in range(GROUP):
        re = step[:ROWS_W, i * LANES : (i + 1) * LANES]
        im = step[ROWS_W:, i * LANES : (i + 1) * LANES]
        rows.append(jnp.concatenate([re * cos + im * sin, im * cos - re * sin], 1))
    return jnp.concatenate(rows, 0)


def spectrum_kernel(h_ref, outer_ref, twist_ref, fwd_ref, out_ref, wide_ref):
    channels = h_ref.shape[0]
    for q in range(TILES):
        wide_ref[pl.ds(q, channels, stride=TILES), :] = h_ref[:, q * LANES : (q + 1) * LANES]

    @pl.loop(0, channels // GROUP)
    def _(step):
        pieces = []
        for i in range(GROUP):
            hi, lo = split(wide_ref[pl.ds((step * GROUP + i) * TILES, TILES), :])
            pieces.append(jnp.concatenate([hi, hi, lo], 0))
        first = mm(outer_ref[...], jnp.concatenate(pieces, 1))
        out_ref[pl.ds(step * GROUP * ROWS_W, GROUP * ROWS_W), :] = mm3(
            twisted(first, twist_ref), fwd_ref
        )


def spectrum(h, interpret=False):
    outer3, twist, fwd, _, _ = tables()
    return pl.pallas_call(
        spectrum_kernel,
        out_shape=jax.ShapeDtypeStruct((h.shape[0] * ROWS_W, 256), F32),
        scratch_shapes=[pltpu.VMEM((h.shape[0] * TILES, LANES), F32)],
        compiler_params=pltpu.CompilerParams(vmem_limit_bytes=BIG),
        interpret=interpret,
        name="spectrum",
    )(h, outer3, twist, fwd)


def convolve_kernel(
    proj_ref,
    ids_ref,
    factor_ref,
    taps_ref,
    spec_ref,
    outer_ref,
    twist_ref,
    fwd_ref,
    bwd_ref,
    inv_ref,
    out_ref,
    left_ref,
    wide_ref,
    gate_ref,
    mix_ref,
    y_ref,
):
    channels = 32
    for s in range(16):
        left_ref[0:96, s * 128 : (s + 1) * 128] = proj_ref[s, :, :128]
        left_ref[96:192, s * 128 : (s + 1) * 128] = proj_ref[s, :, 128:]
    vocab = lax.broadcasted_iota(jnp.int32, (1024, FRAME), 0)

    @pl.loop(0, 8)
    def _(z):
        ids = ids_ref[z]
        for i in range(4):
            hot = jnp.concatenate(
                [
                    (vocab == ids[i : i + 1]).astype(BF16),
                    (vocab == ids[4 + i : 5 + i]).astype(BF16),
                ],
                0,
            )
            both = mm(left_ref[...], hot)
            value = both[:96] + both[96:]
            for half in range(2):
                wide_ref[pl.ds(z * 8 + 2 * i + half, 96, stride=TILES), :] = value[
                    :, half * LANES : (half + 1) * LANES
                ]

    tap_row = lax.broadcasted_iota(jnp.int32, (LANES, LANES), 0)
    tap_col = lax.broadcasted_iota(jnp.int32, (LANES, LANES), 1)
    rows = 16 * TILES
    first_tile = lax.broadcasted_iota(jnp.int32, (rows, LANES), 0) % TILES == 0
    scale = jnp.concatenate([factor_ref[...]] * 16, 0)

    def filtered(k, g):
        taps = jnp.broadcast_to(taps_ref[2 * k + g : 2 * k + g + 1, :], (LANES, LANES))
        turned = pltpu.roll(taps, 0, 1, stride=1, stride_axis=0)
        both = jnp.concatenate(
            [
                jnp.where(tap_col >= tap_row, turned, 0.0),
                jnp.where(tap_col < tap_row, turned, 0.0),
            ],
            1,
        ).astype(BF16)
        start = (2 * k + g) * rows
        x = (wide_ref[start : start + rows, :] * scale).astype(BF16)
        parts = mm(x, both)
        carried = jnp.where(first_tile, 0.0, pltpu.roll(parts[:, LANES:], 1, 0))
        return (parts[:, :LANES] + carried).astype(BF16)

    for g in range(2):
        gate_ref[g * rows : (g + 1) * rows, :] = filtered(0, g)
        left = filtered(1, g).astype(F32)
        mix_ref[g * rows : (g + 1) * rows, :] = (left * filtered(2, g).astype(F32)).astype(BF16)

    @pl.loop(0, channels // GROUP)
    def _(step):
        pieces = []
        for i in range(GROUP):
            x = mix_ref[pl.ds((step * GROUP + i) * TILES, TILES), :]
            pieces.append(jnp.concatenate([x, x], 0))
        first = mm(outer_ref[:, : 2 * TILES], jnp.concatenate(pieces, 1))
        spec = mm3(twisted(first, twist_ref), fwd_ref)
        other = spec_ref[pl.ds(step * GROUP * ROWS_W, GROUP * ROWS_W), :]
        re, im = spec[:, :LANES], spec[:, LANES:]
        ore, oim = other[:, :LANES], other[:, LANES:]
        back = mm3(jnp.concatenate([re * ore - im * oim, re * oim + im * ore], 1), bwd_ref)
        cos, sin = twist_ref[0], twist_ref[1]
        columns = []
        for i in range(GROUP):
            bre = back[i * ROWS_W : (i + 1) * ROWS_W, :LANES]
            bim = back[i * ROWS_W : (i + 1) * ROWS_W, LANES:]
            undone = jnp.concatenate([bre * cos - bim * sin, bim * cos + bre * sin], 0)
            hi, lo = split(undone)
            columns.append(jnp.concatenate([hi, hi, lo], 0))
        result = mm(inv_ref[...], jnp.concatenate(columns, 1))
        for i in range(GROUP):
            at = pl.ds((step * GROUP + i) * TILES, TILES)
            conv = result[:, i * LANES : (i + 1) * LANES].astype(BF16).astype(F32)
            y_ref[at, :] = gate_ref[at, :].astype(F32) * conv

    for q in range(TILES):
        out_ref[q // 8, :, (q % 8) * LANES : (q % 8 + 1) * LANES] = y_ref[
            pl.ds(q, channels, stride=TILES), :
        ].astype(BF16)


def convolve(proj, ids, factor, taps, spec, interpret=False):
    outer3, twist, fwd, bwd, inv3 = tables()
    return pl.pallas_call(
        convolve_kernel,
        out_shape=jax.ShapeDtypeStruct((8, 32, 1024), BF16),
        scratch_shapes=[
            pltpu.VMEM((192, 2048), BF16),
            pltpu.VMEM((96 * TILES, LANES), F32),
            pltpu.VMEM((32 * TILES, LANES), BF16),
            pltpu.VMEM((32 * TILES, LANES), BF16),
            pltpu.VMEM((32 * TILES, LANES), F32),
        ],
        compiler_params=pltpu.CompilerParams(vmem_limit_bytes=BIG),
        interpret=interpret,
        name="convolve",
    )(proj, ids, factor, taps, spec, outer3, twist, fwd, bwd, inv3)


def heads_kernel(hy_ref, w_ref, out_ref, state_ref, acc_ref):
    step = pl.program_id(0)

    @pl.when(step == 0)
    def _():
        acc_ref[...] = jnp.zeros_like(acc_ref)

    x = hy_ref[0]
    for k in range(3):
        acc_ref[k] += lax.dot_general(
            w_ref[k], x, (((0,), (0,)), ((), ())), preferred_element_type=F32
        )

    @pl.when(step == pl.num_programs(0) - 1)
    def _():
        heads = acc_ref[...].astype(BF16)
        out_ref[...] = heads
        for b in range(heads.shape[2] // BLOCK):
            at = slice(b * BLOCK, (b + 1) * BLOCK)
            state_ref[b] = lax.dot_general(
                heads[1, :, at],
                heads[2, :, at],
                (((1,), (1,)), ((), ())),
                preferred_element_type=F32,
            )


def heads_of(hyena, w, interpret=False):
    chans, depth, length = hyena.shape
    return pl.pallas_call(
        heads_kernel,
        grid=(chans,),
        in_specs=[
            pl.BlockSpec((1, depth, length), lambda c: (c, 0, 0)),
            pl.BlockSpec((3, depth, HD), lambda c: (0, c, 0)),
        ],
        out_specs=[
            pl.BlockSpec((3, HD, length), lambda c: (0, 0, 0)),
            pl.BlockSpec((length // BLOCK, HD, HD), lambda c: (0, 0, 0)),
        ],
        out_shape=(
            jax.ShapeDtypeStruct((3, HD, length), BF16),
            jax.ShapeDtypeStruct((length // BLOCK, HD, HD), F32),
        ),
        scratch_shapes=[pltpu.VMEM((3, HD, length), F32)],
        compiler_params=pltpu.CompilerParams(vmem_limit_bytes=BIG),
        interpret=interpret,
        name="heads",
    )(hyena, w)


def attention_kernel(heads_ref, state_ref, parts_ref, mine_ref, out_ref):
    mine = mine_ref[0]
    incoming = jnp.zeros((HD, HD), F32)
    for z in range(parts_ref.shape[0]):
        incoming = incoming + jnp.where(z < mine, parts_ref[z, 0] + parts_ref[z, 1], 0.0)
    length = heads_ref.shape[2]
    row = lax.broadcasted_iota(jnp.int32, (BLOCK, BLOCK), 0)
    column = lax.broadcasted_iota(jnp.int32, (BLOCK, BLOCK), 1)
    place = lax.broadcasted_iota(jnp.int32, (BLOCK, HD), 0)
    for b in range(length // BLOCK):
        at = slice(b * BLOCK, (b + 1) * BLOCK)
        queries = jnp.transpose(heads_ref[0, :, at].astype(F32)).astype(BF16)
        scores = mm(queries, heads_ref[1, :, at])
        scores = jnp.where(row >= column, scores, 0.0).astype(BF16)
        inside = lax.dot_general(
            scores, heads_ref[2, :, at], (((1,), (1,)), ((), ())), preferred_element_type=F32
        )
        carried = mm(queries, incoming.astype(BF16))
        position = mine * length + b * BLOCK + place + 1
        divisor = jnp.sqrt((position * HD).astype(F32))
        out_ref[at, :] = ((inside + carried) / divisor).astype(BF16)
        incoming = incoming + state_ref[b]


def attention(heads, state, parts, mine, interpret=False):
    vmem = pl.BlockSpec(memory_space=pltpu.VMEM)
    return pl.pallas_call(
        attention_kernel,
        in_specs=[vmem, vmem, vmem, pl.BlockSpec(memory_space=pltpu.SMEM)],
        out_shape=jax.ShapeDtypeStruct((heads.shape[2], HD), BF16),
        compiler_params=pltpu.CompilerParams(vmem_limit_bytes=BIG),
        interpret=interpret,
        name="attention",
    )(heads, state, parts, mine)


def here():
    return lax.axis_index("seq"), lax.axis_index("chan"), lax.axis_index("rep")


def greet(peers):
    barrier = pltpu.get_barrier_semaphore()
    for peer in peers:
        pl.semaphore_signal(barrier, inc=1, device_id=peer, device_id_type=MESH)
    pl.semaphore_wait(barrier, len(peers))


def push(src, dst, sems, index, peer):
    copy = pltpu.make_async_remote_copy(
        src_ref=src,
        dst_ref=dst,
        send_sem=sems[0].at[index],
        recv_sem=sems[1].at[index],
        device_id=peer,
        device_id_type=MESH,
    )
    copy.start()
    return copy


def comm_call(kernel, outs, copies, locals_, collective_id, name, *args):
    return pl.pallas_call(
        kernel,
        in_specs=[ANY] * len(args),
        out_specs=[ANY] * len(outs) if isinstance(outs, tuple) else ANY,
        out_shape=outs,
        scratch_shapes=[
            pltpu.SemaphoreType.DMA((copies,)),
            pltpu.SemaphoreType.DMA((copies,)),
            pltpu.SemaphoreType.DMA((locals_,)),
        ],
        compiler_params=pltpu.CompilerParams(collective_id=collective_id, has_side_effects=True),
        name=name,
    )(*args)


def share_kernel(rows_ref, side_ref, ids_ref, rows_out, side_out, ids_out, send, recv, own):
    z, c, r = here()
    sems = (send, recv)
    plane = [(z, lax.rem(c + j, 16), r) for j in range(1, 16)]
    line = [(lax.rem(z + j, 8), c, r) for j in range(1, 8)]
    greet(plane + line)
    copies = []
    for j, peer in enumerate(plane):
        copies.append(push(rows_ref, rows_out.at[c], sems, j, peer))
        copies.append(push(side_ref, side_out.at[c], sems, 15 + j, peer))
    for j, peer in enumerate(line):
        copies.append(push(ids_ref, ids_out.at[z], sems, 30 + j, peer))
    mine = [
        pltpu.make_async_copy(rows_ref, rows_out.at[c], own.at[0]),
        pltpu.make_async_copy(side_ref, side_out.at[c], own.at[1]),
        pltpu.make_async_copy(ids_ref, ids_out.at[z], own.at[2]),
    ]
    for copy in mine:
        copy.start()
    for copy in mine + copies:
        copy.wait()


def deal_kernel(proj_ref, factor_ref, proj_out, factor_out, send, recv, own):
    z, c, r = here()
    sems = (send, recv)
    slot = r * 8 + z
    peers = []
    for flip in range(2):
        for j in range(8):
            if flip or j:
                peers.append((lax.rem(z + j, 8), c, lax.rem(r + flip, 2)))
    greet(peers)

    def piece(to):
        return proj_ref.at[:, pl.ds(pl.multiple_of(to * 32, 32), 32), :]

    copies = []
    for index, peer in enumerate(peers):
        copies.append(push(piece(peer[0]), proj_out.at[slot], sems, index, peer))
    for j in range(7):
        copies.append(push(factor_ref, factor_out.at[z], sems, 15 + j, peers[j]))
    mine = [
        pltpu.make_async_copy(piece(z), proj_out.at[slot], own.at[0]),
        pltpu.make_async_copy(factor_ref, factor_out.at[z], own.at[1]),
    ]
    for copy in mine:
        copy.start()
    for copy in mine + copies:
        copy.wait()


def turn_kernel(y_ref, out_ref, send, recv, own):
    z, c, r = here()
    peers = [(lax.rem(z + j, 8), c, r) for j in range(1, 8)]
    greet(peers)
    place = out_ref.at[pl.ds(pl.multiple_of(z * 32, 32), 32), :]
    copies = [
        push(y_ref.at[peer[0]], place, (send, recv), j, peer) for j, peer in enumerate(peers)
    ]
    mine = pltpu.make_async_copy(y_ref.at[z], place, own.at[0])
    mine.start()
    mine.wait()
    for copy in copies:
        copy.wait()


def gather_kernel(x_ref, out_ref, send, recv, own):
    z, c, r = here()
    y, x = c // 4, lax.rem(c, 4)
    sems = (send, recv)

    def chan(at_x, at_y):
        return lax.rem(at_y + 8, 4) * 4 + lax.rem(at_x + 8, 4)

    def device(at_x, at_y):
        return (z, chan(at_x, at_y), r)

    greet([device(x + 1, y), device(x - 1, y), device(x, y + 1), device(x, y - 1)])
    half = x_ref.shape[0] // 2
    quarter = half // 2
    index = [0]
    sent = []

    def send_block(lead, along, across, part, direction, phase):
        axes = (0, 1) if lead == 0 else (1, 0)
        offset = [0, 0]
        offset[axes[0]], offset[axes[1]] = along, across
        origin = chan(x - offset[0], y - offset[1])
        step = [0, 0]
        step[axes[phase]] = direction
        target = device(x + step[0], y + step[1])
        start = lead * half + (0 if part is None else part * quarter)
        size = half if part is None else quarter
        rows = pl.ds(start, size)
        dst = out_ref.at[origin, rows, :]
        src = x_ref.at[rows, :] if along == 0 and across == 0 else dst
        number = index[0]
        index[0] += 1
        copy = push(src, dst, sems, number, target)
        sent.append(copy)
        came = [offset[0] + step[0], offset[1] + step[1]]
        landed = out_ref.at[chan(x - came[0], y - came[1]), rows, :]
        arrival = pltpu.make_async_remote_copy(
            src_ref=landed,
            dst_ref=landed,
            send_sem=send.at[number],
            recv_sem=recv.at[number],
            device_id=target,
            device_id_type=MESH,
        )
        return arrival

    mine = pltpu.make_async_copy(x_ref, out_ref.at[c], own.at[0])
    first = {}
    second = {}
    for lead in range(2):
        for d in (1, -1):
            first[lead, d] = send_block(lead, 0, 0, None, d, 0)
    for lead in range(2):
        for d in (1, -1):
            second[lead, 0, d] = send_block(lead, 0, 0, None, d, 1)
    mine.start()
    turned = {}
    for d in (1, -1):
        for lead in range(2):
            first[lead, d].wait_recv()
            turned[lead, d] = send_block(lead, d, 0, 0 if d == 1 else 1, d, 0)
            for e in (1, -1):
                second[lead, d, e] = send_block(lead, d, 0, None, e, 1)
    last = []

    def onward(lead, along):
        for e in (1, -1):
            second[lead, along, e].wait_recv()
            last.append(send_block(lead, along, e, 0 if e == 1 else 1, e, 1))

    for lead in range(2):
        onward(lead, 0)
    for lead in range(2):
        turned[lead, 1].wait_recv()
        turned[lead, -1].wait_recv()
        for e in (1, -1):
            second[lead, 2, e] = send_block(lead, 2, 0, None, e, 1)
    for along in (1, -1, 2):
        for lead in range(2):
            onward(lead, along)
    for arrival in last:
        arrival.wait_recv()
    for copy in sent:
        copy.wait_send()
    mine.wait()


def states_kernel(state_ref, out_ref, send, recv, own):
    z, c, r = here()
    peers = [(lax.rem(z + j, 8), c, r) for j in range(1, 8)]
    greet(peers)
    copies = [
        push(state_ref, out_ref.at[z], (send, recv), j, peer) for j, peer in enumerate(peers)
    ]
    mine = pltpu.make_async_copy(state_ref, out_ref.at[z], own.at[0])
    mine.start()
    mine.wait()
    for copy in copies:
        copy.wait()


def shards(
    fine_codes,
    coarse_codes,
    frame_order,
    emb_fine,
    emb_coarse,
    norm_gain,
    w_hyena,
    short_taps,
    long_filter,
    w_attn,
):
    z, r = lax.axis_index("seq"), lax.axis_index("rep")
    spec = spectrum(long_filter)
    ids, sums = local_ids(fine_codes, coarse_codes, frame_order, emb_fine, emb_coarse)
    fine_rows = lax.dynamic_slice_in_dim(emb_fine, z * 128, 128, 0)
    coarse_rows = lax.dynamic_slice_in_dim(emb_coarse, z * 128, 128, 0)
    rows = jnp.where(r == 0, fine_rows, coarse_rows)
    side = jnp.concatenate(
        [jnp.broadcast_to(norm_gain.astype(F32)[None], (8, 256)), sums], axis=1
    )
    rows_all, side_all, ids_all = comm_call(
        share_kernel,
        (
            jax.ShapeDtypeStruct((16, 128, 256), BF16),
            jax.ShapeDtypeStruct((16, 8, 384), F32),
            jax.ShapeDtypeStruct((8, 8, FRAME), jnp.int32),
        ),
        37,
        3,
        0,
        "share",
        rows,
        side,
        ids,
    )
    proj, factor = project(rows_all, side_all, jnp.transpose(w_hyena, (1, 0, 2)))
    proj_all, factor_all = comm_call(
        deal_kernel,
        (
            jax.ShapeDtypeStruct((16, 3, 32, 256), BF16),
            jax.ShapeDtypeStruct((8, 8, LANES), F32),
        ),
        22,
        2,
        1,
        "deal",
        proj,
        factor,
    )
    taps = lax.dynamic_slice_in_dim(short_taps, z * 2, 2, 1).reshape(6, LANES).astype(F32)
    y = convolve(
        proj_all.reshape(16, 96, 256), ids_all, factor_all.reshape(TILES, LANES), taps, spec
    )
    hyena_out = comm_call(
        turn_kernel, jax.ShapeDtypeStruct((256, 1024), BF16), 7, 1, 2, "turn", y
    )
    hyena_all = comm_call(
        gather_kernel, jax.ShapeDtypeStruct((16, 256, 1024), BF16), 40, 1, 3, "gather", hyena_out
    )
    heads, state = heads_of(hyena_all, jnp.transpose(w_attn, (1, 0, 2)))
    parts = comm_call(
        states_kernel, jax.ShapeDtypeStruct((8, 2, HD, HD), F32), 7, 1, 4, "states", state
    )
    attn_out = attention(heads, state, parts, z.astype(jnp.int32)[None])
    return (hyena_out, attn_out)


def solution(mesh):
    return jax.shard_map(
        shards,
        mesh=mesh,
        in_specs=(
            P(("rep", "seq")),
            P(("rep", "seq")),
            P(),
            P(None, "chan"),
            P(None, "chan"),
            P("chan"),
            P(None, None, "chan"),
            P(None, "chan", None),
            P(("chan", "seq"), None),
            P(None, None, "chan"),
        ),
        out_specs=(P("chan", ("rep", "seq")), P(("rep", "seq"), "chan")),
        check_vma=False,
    )
```

profile of v0, /device:TPU:32, one launch (start us, length us, event | category | flops | bytes accessed | tf_op | source)
XLA Modules:
  0.0 205.2 jit_solution(14541799335968600093)
XLA Ops:
  0.6 0.7 pad.clone
  1.3 0.7 dynamic-slice_convert_fusion
  2.0 0.6 reshape.24.taps_ref
  2.6 1.3 reshape.20.fine_ref
  3.9 3.3 %local_ids.1 = (s32[8,256]{1,0:T(8,128)}, f32[8,128]{1,0:T(8,128)}) custom-call(s32[4,256]{1,0:T(4,128)} %reshape.20.fine_ref, s32[4,128]{1,0:T(4,128)} %bitcast.11, s32[1,256]{1,0:T(1,128)} %bitcast.12, bf16[1024,256]{1,0:T(8,128)(2,1)} %emb_fine_ref.1, bf16[1024,256]{1,0:T(8,128)(2,1)} %emb_coarse_ref.1), custom_call_target="tpu_custom_call" | custom-call | tf_op jit(solution)/shard_map/local_ids/pallas_call | solution.py:105
  7.2 1.3 pad_maximum_fusion.side_ref
  8.5 1.5 dynamic-slice_select_fusion.rows_ref
  10.0 25.2 %share.1 = (bf16[16,128,256]{2,1,0:T(8,128)(2,1)}, f32[16,8,384]{2,1,0:T(8,128)}, s32[8,8,256]{2,1,0:T(8,128)}) custom-call(bf16[128,256]{1,0:T(8,128)(2,1)} %dynamic-slice_select_fusion.rows_ref, f32[8,384]{1,0:T(8,128)} %pad_maximum_fusion.side_ref, s32[8,256]{1,0:T(8,128)} %get-tuple-element.14.ids_ref), custom_call_target="tpu_custom_call" | custom-call | tf_op jit(solution)/shard_map/share/pallas_call | solution.py:437
  35.2 6.2 %project.1 = (bf16[3,256,256]{2,1,0:T(8,128)(2,1)}, f32[8,128]{1,0:T(8,128)}) custom-call(bf16[16,128,256]{2,1,0:T(8,128)(2,1)} %get-tuple-element.15.rows_ref, f32[16,8,384]{2,1,0:T(8,128)} %get-tuple-element.16.side_ref, bf16[3,4096,256]{2,1,0:T(8,128)(2,1)} %bitcast.7), custom_call_target="tpu_custom_call" | custom-call | tf_op jit(solution)/shard_map/project/pallas_call | solution.py:141
  41.4 25.1 %deal.1 = (bf16[16,3,32,256]{3,2,1,0:T(8,128)(2,1)}, f32[8,8,128]{2,1,0:T(8,128)}) custom-call(bf16[3,256,256]{2,1,0:T(8,128)(2,1)} %get-tuple-element.17.proj_ref, f32[8,128]{1,0:T(8,128)} %get-tuple-element.18.factor_ref), custom_call_target="tpu_custom_call" | custom-call | tf_op jit(solution)/shard_map/deal/pallas_call | solution.py:437
  66.5 7.2 %spectrum.1.spec_ref = f32[2304,256]{1,0:T(8,128)} custom-call(f32[32,8192]{1,0:T(8,128)} %h_ref.1, bf16[144,192]{1,0:T(8,128)(2,1)} %constant.30.clone.outer_ref, f32[2,72,128]{2,1,0:T(8,128)} %constant.31.clone.twist_ref, bf16[2,256,256]{2,1,0:T(8,128)(2,1)} %constant.32.clone.fwd_ref), custom_call_target="tpu_custom_call" | custom-call | tf_op jit(solution)/shard_map/spectrum/pallas_call | solution.py:196
  73.7 22.5 %convolve.1.y_ref = bf16[8,32,1024]{2,1,0:T(8,128)(2,1)} custom-call(bf16[16,96,256]{2,1,0:T(8,128)(2,1)} %bitcast.9, s32[8,8,256]{2,1,0:T(8,128)} %get-tuple-element.20.ids_ref, f32[64,128]{1,0:T(8,128)} %bitcast.10, f32[6,128]{1,0:T(8,128)} %reshape.24.taps_ref, f32[2304,256]{1,0:T(8,128)} %spectrum.1.spec_ref, bf16[144,192]{1,0:T(8,128)(2,1)} %constant.30.clone.outer_ref, ...), custom_call_target="tpu_custom_call" | custom-call | tf_op jit(solution)/shard_map/convolve/pallas_call | solution.py:309
  96.3 17.3 %turn.1.x_ref = bf16[256,1024]{1,0:T(8,128)(2,1)} custom-call(bf16[8,32,1024]{2,1,0:T(8,128)(2,1)} %convolve.1.y_ref), custom_call_target="tpu_custom_call" | custom-call | tf_op jit(solution)/shard_map/turn/pallas_call | solution.py:437
  113.6 48.8 %gather.1.hy_ref = bf16[16,256,1024]{2,1,0:T(8,128)(2,1)} custom-call(bf16[256,1024]{1,0:T(8,128)(2,1)} %turn.1.x_ref), custom_call_target="tpu_custom_call" | custom-call | tf_op jit(solution)/shard_map/gather/pallas_call | solution.py:437
  162.4 0.0 copy-start
  162.4 14.2 %heads.1 = (bf16[3,128,1024]{2,1,0:T(8,128)(2,1)}, f32[2,128,128]{2,1,0:T(8,128)}) custom-call(bf16[16,256,1024]{2,1,0:T(8,128)(2,1)} %gather.1.hy_ref, bf16[3,4096,128]{2,1,0:T(8,128)(2,1)} %bitcast.8), custom_call_target="tpu_custom_call" | custom-call | tf_op jit(solution)/shard_map/heads/pallas_call | solution.py:354
  176.5 24.8 %states.1.parts_ref = f32[8,2,128,128]{3,2,1,0:T(8,128)} custom-call(f32[2,128,128]{2,1,0:T(8,128)} %get-tuple-element.23.state_ref), custom_call_target="tpu_custom_call" | custom-call | tf_op jit(solution)/shard_map/states/pallas_call | solution.py:437
  201.3 3.1 %attention.1 = bf16[1024,128]{1,0:T(8,128)(2,1)} custom-call(bf16[3,128,1024]{2,1,0:T(8,128)(2,1)} %get-tuple-element.22.heads_ref, f32[2,128,128]{2,1,0:T(8,128)} %get-tuple-element.23.state_ref, f32[8,2,128,128]{3,2,1,0:T(8,128)} %states.1.parts_ref, s32[1]{0:T(128)} %bitcast.6.mine_ref), custom_call_target="tpu_custom_call" | custom-call | tf_op jit(solution)/shard_map/attention/pallas_call | solution.py:402
  204.4 0.0 copy-done
  204.4 0.8 copy.18
Async XLA Ops:
  162.4 42.0 %copy-start = (bf16[256,1024]{1,0:T(8,128)(2,1)S(1)}, bf16[256,1024]{1,0:T(8,128)(2,1)}, u32[]{:S(2)}) copy-start(bf16[256,1024]{1,0:T(8,128)(2,1)} %turn.1.x_ref) | copy-start | bytes 1572868
where the time goes:
time: 208 us; the launch traced here: 205 us
  Pallas kernels  198 us (95%)
  other arithmetic  3.5 us (2%)
  local copies, waits for them, and re-layouts  3.34 us (2%)
    pallas_call x5, Pallas kernels, comm_call(): pl.pallas_call(kernel, in_specs=[ANY] * len(args), out_specs=[ANY] * len(...  141 us
    pallas_call x1, Pallas kernels, convolve(): pl.pallas_call(convolve_kernel, out_shape=jax.ShapeDtypeStruct((8, 32, 10...  22.5 us
    pallas_call x1, Pallas kernels, heads_of(): pl.pallas_call(heads_kernel, grid=(chans,), in_specs=[pl.BlockSpec((1, de...  14.2 us
    pallas_call x1, Pallas kernels, spectrum(): pl.pallas_call(spectrum_kernel, out_shape=jax.ShapeDtypeStruct((h.shape[0...  7.21 us
    pallas_call x1, Pallas kernels, project(): pl.pallas_call(project_kernel, grid=(3,), in_specs=[pl.BlockSpec(rows.sha...  6.16 us

commit v1 on v0

--- a/solution.py
+++ b/solution.py
@@ -71,7 +71,7 @@
     return mm(hi, table[0]) + (mm(lo, table[0]) + mm(hi, table[1]))
 
 
-def ids_kernel(fine_ref, coarse_ref, order_ref, emb_fine_ref, emb_coarse_ref, ids_ref, sums_ref):
+def local_sums(fine_ref, coarse_ref, order_ref, emb_fine_ref, emb_coarse_ref, ids_ref, side_ref):
     order = order_ref[...]
     row = lax.broadcasted_iota(jnp.int32, (FRAME, FRAME), 0)
     pick = (row == order).astype(BF16)
@@ -97,21 +97,8 @@
         )
         rows = rows.astype(BF16).astype(F32)
         total = jnp.sum(rows * rows, axis=0, keepdims=True)
-        sums_ref[2 * frame : 2 * frame + 1, :] = total[:, :LANES]
-        sums_ref[2 * frame + 1 : 2 * frame + 2, :] = total[:, LANES:]
-
-
-def local_ids(fine, coarse, order, emb_fine, emb_coarse, interpret=False):
-    return pl.pallas_call(
-        ids_kernel,
-        out_shape=(
-            jax.ShapeDtypeStruct((8, FRAME), jnp.int32),
-            jax.ShapeDtypeStruct((8, LANES), F32),
-        ),
-        compiler_params=pltpu.CompilerParams(vmem_limit_bytes=BIG),
-        interpret=interpret,
-        name="local_ids",
-    )(fine.reshape(4, FRAME), coarse.reshape(4, FRAME // 2), order[None], emb_fine, emb_coarse)
+        side_ref[2 * frame : 2 * frame + 1, FRAME:] = total[:, :LANES]
+        side_ref[2 * frame + 1 : 2 * frame + 2, FRAME:] = total[:, LANES:]
 
 
 def project_kernel(rows_ref, side_ref, w_ref, out_ref, factor_ref, x_ref):
@@ -189,18 +176,6 @@
         out_ref[pl.ds(step * GROUP * ROWS_W, GROUP * ROWS_W), :] = mm3(
             twisted(first, twist_ref), fwd_ref
         )
-
-
-def spectrum(h, interpret=False):
-    outer3, twist, fwd, _, _ = tables()
-    return pl.pallas_call(
-        spectrum_kernel,
-        out_shape=jax.ShapeDtypeStruct((h.shape[0] * ROWS_W, 256), F32),
-        scratch_shapes=[pltpu.VMEM((h.shape[0] * TILES, LANES), F32)],
-        compiler_params=pltpu.CompilerParams(vmem_limit_bytes=BIG),
-        interpret=interpret,
-        name="spectrum",
-    )(h, outer3, twist, fwd)
 
 
 def convolve_kernel(
@@ -322,93 +297,6 @@
     )(proj, ids, factor, taps, spec, outer3, twist, fwd, bwd, inv3)
 
 
-def heads_kernel(hy_ref, w_ref, out_ref, state_ref, acc_ref):
-    step = pl.program_id(0)
-
-    @pl.when(step == 0)
-    def _():
-        acc_ref[...] = jnp.zeros_like(acc_ref)
-
-    x = hy_ref[0]
-    for k in range(3):
-        acc_ref[k] += lax.dot_general(
-            w_ref[k], x, (((0,), (0,)), ((), ())), preferred_element_type=F32
-        )
-
-    @pl.when(step == pl.num_programs(0) - 1)
-    def _():
-        heads = acc_ref[...].astype(BF16)
-        out_ref[...] = heads
-        for b in range(heads.shape[2] // BLOCK):
-            at = slice(b * BLOCK, (b + 1) * BLOCK)
-            state_ref[b] = lax.dot_general(
-                heads[1, :, at],
-                heads[2, :, at],
-                (((1,), (1,)), ((), ())),
-                preferred_element_type=F32,
-            )
-
-
-def heads_of(hyena, w, interpret=False):
-    chans, depth, length = hyena.shape
-    return pl.pallas_call(
-        heads_kernel,
-        grid=(chans,),
-        in_specs=[
-            pl.BlockSpec((1, depth, length), lambda c: (c, 0, 0)),
-            pl.BlockSpec((3, depth, HD), lambda c: (0, c, 0)),
-        ],
-        out_specs=[
-            pl.BlockSpec((3, HD, length), lambda c: (0, 0, 0)),
-            pl.BlockSpec((length // BLOCK, HD, HD), lambda c: (0, 0, 0)),
-        ],
-        out_shape=(
-            jax.ShapeDtypeStruct((3, HD, length), BF16),
-            jax.ShapeDtypeStruct((length // BLOCK, HD, HD), F32),
-        ),
-        scratch_shapes=[pltpu.VMEM((3, HD, length), F32)],
-        compiler_params=pltpu.CompilerParams(vmem_limit_bytes=BIG),
-        interpret=interpret,
-        name="heads",
-    )(hyena, w)
-
-
-def attention_kernel(heads_ref, state_ref, parts_ref, mine_ref, out_ref):
-    mine = mine_ref[0]
-    incoming = jnp.zeros((HD, HD), F32)
-    for z in range(parts_ref.shape[0]):
-        incoming = incoming + jnp.where(z < mine, parts_ref[z, 0] + parts_ref[z, 1], 0.0)
-    length = heads_ref.shape[2]
-    row = lax.broadcasted_iota(jnp.int32, (BLOCK, BLOCK), 0)
-    column = lax.broadcasted_iota(jnp.int32, (BLOCK, BLOCK), 1)
-    place = lax.broadcasted_iota(jnp.int32, (BLOCK, HD), 0)
-    for b in range(length // BLOCK):
-        at = slice(b * BLOCK, (b + 1) * BLOCK)
-        queries = jnp.transpose(heads_ref[0, :, at].astype(F32)).astype(BF16)
-        scores = mm(queries, heads_ref[1, :, at])
-        scores = jnp.where(row >= column, scores, 0.0).astype(BF16)
-        inside = lax.dot_general(
-            scores, heads_ref[2, :, at], (((1,), (1,)), ((), ())), preferred_element_type=F32
-        )
-        carried = mm(queries, incoming.astype(BF16))
-        position = mine * length + b * BLOCK + place + 1
-        divisor = jnp.sqrt((position * HD).astype(F32))
-        out_ref[at, :] = ((inside + carried) / divisor).astype(BF16)
-        incoming = incoming + state_ref[b]
-
-
-def attention(heads, state, parts, mine, interpret=False):
-    vmem = pl.BlockSpec(memory_space=pltpu.VMEM)
-    return pl.pallas_call(
-        attention_kernel,
-        in_specs=[vmem, vmem, vmem, pl.BlockSpec(memory_space=pltpu.SMEM)],
-        out_shape=jax.ShapeDtypeStruct((heads.shape[2], HD), BF16),
-        compiler_params=pltpu.CompilerParams(vmem_limit_bytes=BIG),
-        interpret=interpret,
-        name="attention",
-    )(heads, state, parts, mine)
-
-
 def here():
     return lax.axis_index("seq"), lax.axis_index("chan"), lax.axis_index("rep")
 
@@ -433,31 +321,50 @@
     return copy
 
 
-def comm_call(kernel, outs, copies, locals_, collective_id, name, *args):
-    return pl.pallas_call(
-        kernel,
-        in_specs=[ANY] * len(args),
-        out_specs=[ANY] * len(outs) if isinstance(outs, tuple) else ANY,
-        out_shape=outs,
-        scratch_shapes=[
-            pltpu.SemaphoreType.DMA((copies,)),
-            pltpu.SemaphoreType.DMA((copies,)),
-            pltpu.SemaphoreType.DMA((locals_,)),
-        ],
-        compiler_params=pltpu.CompilerParams(collective_id=collective_id, has_side_effects=True),
-        name=name,
-    )(*args)
-
-
-def share_kernel(rows_ref, side_ref, ids_ref, rows_out, side_out, ids_out, send, recv, own):
+def share_kernel(
+    fine_ref,
+    coarse_ref,
+    order_ref,
+    emb_fine_ref,
+    emb_coarse_ref,
+    gain_ref,
+    filter_ref,
+    outer_ref,
+    twist_ref,
+    fwd_ref,
+    rows_out,
+    side_out,
+    ids_out,
+    spec_ref,
+    rows_ref,
+    side_ref,
+    ids_ref,
+    wide_ref,
+    send,
+    recv,
+    own,
+):
     z, c, r = here()
     sems = (send, recv)
     plane = [(z, lax.rem(c + j, 16), r) for j in range(1, 16)]
     line = [(lax.rem(z + j, 8), c, r) for j in range(1, 8)]
+    at = pl.ds(pl.multiple_of(z * 128, 128), 128)
+
+    @pl.when(r == 0)
+    def _():
+        rows_ref[...] = emb_fine_ref[at, :]
+
+    @pl.when(r != 0)
+    def _():
+        rows_ref[...] = emb_coarse_ref[at, :]
+
     greet(plane + line)
     copies = []
     for j, peer in enumerate(plane):
         copies.append(push(rows_ref, rows_out.at[c], sems, j, peer))
+    side_ref[:, :FRAME] = jnp.broadcast_to(gain_ref[...].astype(F32), (8, FRAME))
+    local_sums(fine_ref, coarse_ref, order_ref, emb_fine_ref, emb_coarse_ref, ids_ref, side_ref)
+    for j, peer in enumerate(plane):
         copies.append(push(side_ref, side_out.at[c], sems, 15 + j, peer))
     for j, peer in enumerate(line):
         copies.append(push(ids_ref, ids_out.at[z], sems, 30 + j, peer))
@@ -468,58 +375,131 @@
     ]
     for copy in mine:
         copy.start()
+    spectrum_kernel(filter_ref, outer_ref, twist_ref, fwd_ref, spec_ref, wide_ref)
     for copy in mine + copies:
         copy.wait()
+
+
+def share(fine, coarse, order, emb_fine, emb_coarse, gain, long_filter):
+    outer3, twist, fwd, _, _ = tables()
+    channels = long_filter.shape[0]
+    vmem = pl.BlockSpec(memory_space=pltpu.VMEM)
+    return pl.pallas_call(
+        share_kernel,
+        in_specs=[vmem] * 10,
+        out_specs=[ANY, ANY, ANY, vmem],
+        out_shape=(
+            jax.ShapeDtypeStruct((16, 128, 256), BF16),
+            jax.ShapeDtypeStruct((16, 8, 384), F32),
+            jax.ShapeDtypeStruct((8, 8, FRAME), jnp.int32),
+            jax.ShapeDtypeStruct((channels * ROWS_W, 256), F32),
+        ),
+        scratch_shapes=[
+            pltpu.VMEM((128, 256), BF16),
+            pltpu.VMEM((8, 384), F32),
+            pltpu.VMEM((8, FRAME), jnp.int32),
+            pltpu.VMEM((channels * TILES, LANES), F32),
+            pltpu.SemaphoreType.DMA((37,)),
+            pltpu.SemaphoreType.DMA((37,)),
+            pltpu.SemaphoreType.DMA((3,)),
+        ],
+        compiler_params=pltpu.CompilerParams(
+            collective_id=0, has_side_effects=True, vmem_limit_bytes=BIG
+        ),
+        name="share",
+    )(
+        fine.reshape(4, FRAME),
+        coarse.reshape(4, FRAME // 2),
+        order[None],
+        emb_fine,
+        emb_coarse,
+        gain[None],
+        long_filter,
+        outer3,
+        twist,
+        fwd,
+    )
 
 
 def deal_kernel(proj_ref, factor_ref, proj_out, factor_out, send, recv, own):
     z, c, r = here()
     sems = (send, recv)
     slot = r * 8 + z
-    peers = []
-    for flip in range(2):
-        for j in range(8):
-            if flip or j:
-                peers.append((lax.rem(z + j, 8), c, lax.rem(r + flip, 2)))
-    greet(peers)
+    line = [(lax.rem(z + j, 8), c, r) for j in range(1, 8)]
+    sibling = (z, c, 1 - r)
+    greet(line + [sibling])
 
     def piece(to):
         return proj_ref.at[:, pl.ds(pl.multiple_of(to * 32, 32), 32), :]
 
     copies = []
-    for index, peer in enumerate(peers):
-        copies.append(push(piece(peer[0]), proj_out.at[slot], sems, index, peer))
-    for j in range(7):
-        copies.append(push(factor_ref, factor_out.at[z], sems, 15 + j, peers[j]))
+    for j, peer in enumerate(line):
+        copies.append(push(piece(peer[0]), proj_out.at[slot], sems, j, peer))
+    for j, peer in enumerate(line):
+        copies.append(push(factor_ref, factor_out.at[z], sems, 7 + j, peer))
+    across = [push(piece(z), proj_out.at[slot], sems, 14, sibling)]
     mine = [
         pltpu.make_async_copy(piece(z), proj_out.at[slot], own.at[0]),
         pltpu.make_async_copy(factor_ref, factor_out.at[z], own.at[1]),
     ]
     for copy in mine:
         copy.start()
-    for copy in mine + copies:
+    for j in range(7):
+        copies[j].wait_recv()
+        landed = proj_out.at[r * 8 + lax.rem(z + 7 - j, 8)]
+        across.append(push(landed, landed, sems, 15 + j, sibling))
+    for copy in across + copies[7:]:
+        copy.wait_recv()
+    for copy in across + copies:
+        copy.wait_send()
+    for copy in mine:
         copy.wait()
 
 
-def turn_kernel(y_ref, out_ref, send, recv, own):
-    z, c, r = here()
-    peers = [(lax.rem(z + j, 8), c, r) for j in range(1, 8)]
-    greet(peers)
-    place = out_ref.at[pl.ds(pl.multiple_of(z * 32, 32), 32), :]
-    copies = [
-        push(y_ref.at[peer[0]], place, (send, recv), j, peer) for j, peer in enumerate(peers)
-    ]
-    mine = pltpu.make_async_copy(y_ref.at[z], place, own.at[0])
-    mine.start()
-    mine.wait()
-    for copy in copies:
-        copy.wait()
-
-
-def gather_kernel(x_ref, out_ref, send, recv, own):
+def deal(proj, factor):
+    return pl.pallas_call(
+        deal_kernel,
+        in_specs=[ANY] * 2,
+        out_specs=[ANY] * 2,
+        out_shape=(
+            jax.ShapeDtypeStruct((16, 3, 32, 256), BF16),
+            jax.ShapeDtypeStruct((8, 8, LANES), F32),
+        ),
+        scratch_shapes=[
+            pltpu.SemaphoreType.DMA((22,)),
+            pltpu.SemaphoreType.DMA((22,)),
+            pltpu.SemaphoreType.DMA((2,)),
+        ],
+        compiler_params=pltpu.CompilerParams(collective_id=1, has_side_effects=True),
+        name="deal",
+    )(proj, factor)
+
+
+CHUNKS = 2
+
+
+def tail_kernel(
+    y_ref,
+    w_ref,
+    hyena_ref,
+    attn_ref,
+    wv_ref,
+    x_ref,
+    land_ref,
+    acc_ref,
+    state_ref,
+    parts_ref,
+    prefix_ref,
+    incoming_ref,
+    send,
+    recv,
+    own,
+):
     z, c, r = here()
     y, x = c // 4, lax.rem(c, 4)
     sems = (send, recv)
+    length = x_ref.shape[1]
+    span = length // CHUNKS
 
     def chan(at_x, at_y):
         return lax.rem(at_y + 8, 4) * 4 + lax.rem(at_x + 8, 4)
@@ -527,32 +507,49 @@
     def device(at_x, at_y):
         return (z, chan(at_x, at_y), r)
 
-    greet([device(x + 1, y), device(x - 1, y), device(x, y + 1), device(x, y - 1)])
+    line = [(lax.rem(z + j, 8), c, r) for j in range(1, 8)]
+    weights = pltpu.make_async_copy(w_ref, wv_ref, own.at[0])
+    weights.start()
+    greet(line + [device(x + 1, y), device(x - 1, y), device(x, y + 1), device(x, y - 1)])
+    index = [0]
+    sent = []
+
+    def tell(src, dst, peer):
+        copy = push(src, dst, sems, index[0], peer)
+        index[0] += 1
+        sent.append(copy)
+        return copy
+
+    mine_rows = pl.ds(pl.multiple_of(z * 32, 32), 32)
+    turned = []
+    kept = []
+    for t in range(CHUNKS):
+        at = pl.ds(t * span, span)
+        kept.append(
+            pltpu.make_async_copy(y_ref.at[z, :, at], x_ref.at[mine_rows, at], own.at[1 + t])
+        )
+        kept[-1].start()
+        turned.append([tell(y_ref.at[p[0], :, at], x_ref.at[mine_rows, at], p) for p in line])
     half = x_ref.shape[0] // 2
     quarter = half // 2
-    index = [0]
-    sent = []
-
-    def send_block(lead, along, across, part, direction, phase):
+
+    def send_block(t, lead, along, across, part, direction, phase):
         axes = (0, 1) if lead == 0 else (1, 0)
         offset = [0, 0]
         offset[axes[0]], offset[axes[1]] = along, across
-        origin = chan(x - offset[0], y - offset[1])
         step = [0, 0]
         step[axes[phase]] = direction
         target = device(x + step[0], y + step[1])
         start = lead * half + (0 if part is None else part * quarter)
-        size = half if part is None else quarter
-        rows = pl.ds(start, size)
-        dst = out_ref.at[origin, rows, :]
-        src = x_ref.at[rows, :] if along == 0 and across == 0 else dst
+        rows = pl.ds(start, half if part is None else quarter)
+        at = pl.ds(t * span, span)
+        dst = land_ref.at[chan(x - offset[0], y - offset[1]), rows, at]
+        src = x_ref.at[rows, at] if along == 0 and across == 0 else dst
         number = index[0]
-        index[0] += 1
-        copy = push(src, dst, sems, number, target)
-        sent.append(copy)
+        tell(src, dst, target)
         came = [offset[0] + step[0], offset[1] + step[1]]
-        landed = out_ref.at[chan(x - came[0], y - came[1]), rows, :]
-        arrival = pltpu.make_async_remote_copy(
+        landed = land_ref.at[chan(x - came[0], y - came[1]), rows, at]
+        return pltpu.make_async_remote_copy(
             src_ref=landed,
             dst_ref=landed,
             send_sem=send.at[number],
@@ -560,61 +557,176 @@
             device_id=target,
             device_id_type=MESH,
         )
-        return arrival
-
-    mine = pltpu.make_async_copy(x_ref, out_ref.at[c], own.at[0])
+
     first = {}
     second = {}
-    for lead in range(2):
+    forward = {}
+    pending = []
+
+    def multiply(t, lead, along, across):
+        at = slice(t * span, (t + 1) * span)
+        rows = slice(lead * half, (lead + 1) * half)
+        offset = (along, across) if lead == 0 else (across, along)
+        origin = chan(x - offset[0], y - offset[1])
+        block = x_ref[rows, at] if offset == (0, 0) else land_ref[origin, rows, at]
+        depth = pl.ds(pl.multiple_of(origin * 2 * half + lead * half, half), half)
+        for k in range(3):
+            product = lax.dot_general(
+                wv_ref[k, depth, :], block, (((0,), (0,)), ((), ())), preferred_element_type=F32
+            )
+            if (along, across, lead) == (0, 0, 0):
+                acc_ref[k, :, at] = product
+            else:
+                acc_ref[k, :, at] += product
+
+    def drain(count):
+        for _ in range(min(count, len(pending))):
+            multiply(*pending.pop(0))
+
+    def open_chunk(t):
+        kept[t].wait()
+        for copy in turned[t]:
+            copy.wait_recv()
+        for lead in range(2):
+            for d in (1, -1):
+                first[t, lead, d] = send_block(t, lead, 0, 0, None, d, 0)
+        for lead in range(2):
+            for d in (1, -1):
+                second[t, lead, 0, d] = send_block(t, lead, 0, 0, None, d, 1)
+        for lead in range(2):
+            pending.append((t, lead, 0, 0))
+
+    last = []
+
+    def onward(t, lead, along):
+        for e in (1, -1):
+            second[t, lead, along, e].wait_recv()
+            last.append((t, lead, along, send_block(t, lead, along, e, 0 if e == 1 else 1, e, 1)))
+        for e in (1, -1):
+            pending.append((t, lead, along, e))
+
+    for t in range(CHUNKS):
+        open_chunk(t)
+    weights.wait()
+    back = pltpu.make_async_copy(x_ref, hyena_ref, own.at[CHUNKS + 1])
+    back.start()
+    for t in range(CHUNKS):
         for d in (1, -1):
-            first[lead, d] = send_block(lead, 0, 0, None, d, 0)
-    for lead in range(2):
-        for d in (1, -1):
-            second[lead, 0, d] = send_block(lead, 0, 0, None, d, 1)
-    mine.start()
-    turned = {}
-    for d in (1, -1):
+            for lead in range(2):
+                first[t, lead, d].wait_recv()
+                forward[t, lead, d] = send_block(t, lead, d, 0, 0 if d == 1 else 1, d, 0)
+                for e in (1, -1):
+                    second[t, lead, d, e] = send_block(t, lead, d, 0, None, e, 1)
+                pending.append((t, lead, d, 0))
+        drain(2)
         for lead in range(2):
-            first[lead, d].wait_recv()
-            turned[lead, d] = send_block(lead, d, 0, 0 if d == 1 else 1, d, 0)
+            onward(t, lead, 0)
+            drain(1)
+        for lead in range(2):
+            forward[t, lead, 1].wait_recv()
+            forward[t, lead, -1].wait_recv()
             for e in (1, -1):
-                second[lead, d, e] = send_block(lead, d, 0, None, e, 1)
-    last = []
-
-    def onward(lead, along):
-        for e in (1, -1):
-            second[lead, along, e].wait_recv()
-            last.append(send_block(lead, along, e, 0 if e == 1 else 1, e, 1))
-
-    for lead in range(2):
-        onward(lead, 0)
-    for lead in range(2):
-        turned[lead, 1].wait_recv()
-        turned[lead, -1].wait_recv()
-        for e in (1, -1):
-            second[lead, 2, e] = send_block(lead, 2, 0, None, e, 1)
-    for along in (1, -1, 2):
-        for lead in range(2):
-            onward(lead, along)
-    for arrival in last:
+                second[t, lead, 2, e] = send_block(t, lead, 2, 0, None, e, 1)
+            pending.append((t, lead, 2, 0))
+            drain(1)
+    for t in range(CHUNKS):
+        for along in (1, -1, 2):
+            for lead in range(2):
+                onward(t, lead, along)
+                drain(3)
+    for t, lead, along, arrival in last:
         arrival.wait_recv()
+    for position in range(0, len(last), 2):
+        t, lead, along, _ = last[position]
+        pending.append((t, lead, along, 2))
+    drain(len(pending))
+
+    blocks = length // BLOCK
+    heads = [[acc_ref[k, :, b * BLOCK : (b + 1) * BLOCK].astype(BF16) for b in range(blocks)] for k in range(3)]
+    states = [
+        lax.dot_general(
+            heads[1][b], heads[2][b], (((1,), (1,)), ((), ())), preferred_element_type=F32
+        )
+        for b in range(blocks)
+    ]
+    total = states[0]
+    for b in range(1, blocks):
+        total = total + states[b]
+    state_ref[...] = total.reshape(8, HD // 8, HD)
+    parts_ref[z] = state_ref[z]
+    gathered = [tell(state_ref.at[p[0]], parts_ref.at[z], p) for p in line]
+    row = lax.broadcasted_iota(jnp.int32, (BLOCK, BLOCK), 0)
+    column = lax.broadcasted_iota(jnp.int32, (BLOCK, BLOCK), 1)
+    queries = []
+    inside = []
+
+    def local(b):
+        queries.append(jnp.transpose(heads[0][b].astype(F32)).astype(BF16))
+        scores = mm(queries[b], heads[1][b])
+        scores = jnp.where(row >= column, scores, 0.0).astype(BF16)
+        inside.append(
+            lax.dot_general(
+                scores, heads[2][b], (((1,), (1,)), ((), ())), preferred_element_type=F32
+            )
+        )
+
+    local(0)
+    for copy in gathered:
+        copy.wait_recv()
+    running = jnp.zeros((HD // 8, HD), F32)
+    for step in range(8):
+        prefix_ref[step] = running
+        running = running + parts_ref[step]
+    incoming_ref[z] = prefix_ref[z]
+    dealt = [tell(prefix_ref.at[p[0]], incoming_ref.at[z], p) for p in line]
+    for b in range(1, blocks):
+        local(b)
+    for copy in dealt:
+        copy.wait_recv()
+    earlier = incoming_ref[...].reshape(HD, HD)
+    place = lax.broadcasted_iota(jnp.int32, (BLOCK, HD), 0)
+    for b in range(blocks):
+        carried = mm(queries[b], earlier.astype(BF16))
+        position = z * length + b * BLOCK + place + 1
+        divisor = jnp.sqrt((position * HD).astype(F32))
+        attn_ref[b * BLOCK : (b + 1) * BLOCK, :] = ((inside[b] + carried) / divisor).astype(BF16)
+        earlier = earlier + states[b]
     for copy in sent:
         copy.wait_send()
-    mine.wait()
-
-
-def states_kernel(state_ref, out_ref, send, recv, own):
-    z, c, r = here()
-    peers = [(lax.rem(z + j, 8), c, r) for j in range(1, 8)]
-    greet(peers)
-    copies = [
-        push(state_ref, out_ref.at[z], (send, recv), j, peer) for j, peer in enumerate(peers)
-    ]
-    mine = pltpu.make_async_copy(state_ref, out_ref.at[z], own.at[0])
-    mine.start()
-    mine.wait()
-    for copy in copies:
-        copy.wait()
+    back.wait()
+
+
+def tail(y, w):
+    seqs, channels, length = y.shape
+    depth = seqs * channels
+    vmem = pl.BlockSpec(memory_space=pltpu.VMEM)
+    copies = CHUNKS * (7 + 40) + 14
+    return pl.pallas_call(
+        tail_kernel,
+        in_specs=[ANY, ANY],
+        out_specs=[ANY, vmem],
+        out_shape=(
+            jax.ShapeDtypeStruct((depth, length), BF16),
+            jax.ShapeDtypeStruct((length, HD), BF16),
+        ),
+        scratch_shapes=[
+            pltpu.VMEM(w.shape, BF16),
+            pltpu.VMEM((depth, length), BF16),
+            pltpu.VMEM((16, depth, length), BF16),
+            pltpu.VMEM((3, HD, length), F32),
+            pltpu.VMEM((8, HD // 8, HD), F32),
+            pltpu.VMEM((8, HD // 8, HD), F32),
+            pltpu.VMEM((8, HD // 8, HD), F32),
+            pltpu.VMEM((8, HD // 8, HD), F32),
+            pltpu.SemaphoreType.DMA((copies,)),
+            pltpu.SemaphoreType.DMA((copies,)),
+            pltpu.SemaphoreType.DMA((CHUNKS + 2,)),
+        ],
+        compiler_params=pltpu.CompilerParams(
+            collective_id=2, has_side_effects=True, vmem_limit_bytes=BIG
+        ),
+        name="tail",
+    )(y, w)
 
 
 def shards(
@@ -629,60 +741,17 @@
     long_filter,
     w_attn,
 ):
-    z, r = lax.axis_index("seq"), lax.axis_index("rep")
-    spec = spectrum(long_filter)
-    ids, sums = local_ids(fine_codes, coarse_codes, frame_order, emb_fine, emb_coarse)
-    fine_rows = lax.dynamic_slice_in_dim(emb_fine, z * 128, 128, 0)
-    coarse_rows = lax.dynamic_slice_in_dim(emb_coarse, z * 128, 128, 0)
-    rows = jnp.where(r == 0, fine_rows, coarse_rows)
-    side = jnp.concatenate(
-        [jnp.broadcast_to(norm_gain.astype(F32)[None], (8, 256)), sums], axis=1
-    )
-    rows_all, side_all, ids_all = comm_call(
-        share_kernel,
-        (
-            jax.ShapeDtypeStruct((16, 128, 256), BF16),
-            jax.ShapeDtypeStruct((16, 8, 384), F32),
-            jax.ShapeDtypeStruct((8, 8, FRAME), jnp.int32),
-        ),
-        37,
-        3,
-        0,
-        "share",
-        rows,
-        side,
-        ids,
+    z = lax.axis_index("seq")
+    rows_all, side_all, ids_all, spec = share(
+        fine_codes, coarse_codes, frame_order, emb_fine, emb_coarse, norm_gain, long_filter
     )
     proj, factor = project(rows_all, side_all, jnp.transpose(w_hyena, (1, 0, 2)))
-    proj_all, factor_all = comm_call(
-        deal_kernel,
-        (
-            jax.ShapeDtypeStruct((16, 3, 32, 256), BF16),
-            jax.ShapeDtypeStruct((8, 8, LANES), F32),
-        ),
-        22,
-        2,
-        1,
-        "deal",
-        proj,
-        factor,
-    )
+    proj_all, factor_all = deal(proj, factor)
     taps = lax.dynamic_slice_in_dim(short_taps, z * 2, 2, 1).reshape(6, LANES).astype(F32)
     y = convolve(
         proj_all.reshape(16, 96, 256), ids_all, factor_all.reshape(TILES, LANES), taps, spec
     )
-    hyena_out = comm_call(
-        turn_kernel, jax.ShapeDtypeStruct((256, 1024), BF16), 7, 1, 2, "turn", y
-    )
-    hyena_all = comm_call(
-        gather_kernel, jax.ShapeDtypeStruct((16, 256, 1024), BF16), 40, 1, 3, "gather", hyena_out
-    )
-    heads, state = heads_of(hyena_all, jnp.transpose(w_attn, (1, 0, 2)))
-    parts = comm_call(
-        states_kernel, jax.ShapeDtypeStruct((8, 2, HD, HD), F32), 7, 1, 4, "states", state
-    )
-    attn_out = attention(heads, state, parts, z.astype(jnp.int32)[None])
-    return (hyena_out, attn_out)
+    return tail(y, jnp.transpose(w_attn, (1, 0, 2)))
 
 
 def solution(mesh):

time: 208 us -> 156 us (0.75); the launches traced: 205 us -> 155 us
  Pallas kernels: 198 us -> 147 us
  local copies, waits for them, and re-layouts: 3.34 us -> 6.65 us
  other arithmetic: 3.5 us -> 0.7 us
    pallas_call x9 -> x3, Pallas kernels: 169 us -> 119 us  [the longest x1 75 us: tail(): pl.pallas_call(tail_kernel, in_specs=[ANY, ANY], out_specs=[ANY, vmem], o...]
    unnamed x3 -> x2, local copies, waits for them, and re-layouts: 0.8 us -> 3.54 us
where the time goes in v1:
time: 156 us; the launch traced here: 155 us
  Pallas kernels  147 us (94%)
  local copies, waits for them, and re-layouts  6.65 us (4%)
    pallas_call x1, Pallas kernels, tail(): pl.pallas_call(tail_kernel, in_specs=[ANY, ANY], out_specs=[ANY, vmem], o...  75 us
    pallas_call x1, Pallas kernels, share(): pl.pallas_call(share_kernel, in_specs=[vmem] * 10, out_specs=[ANY, ANY, A...  29.6 us
    pallas_call x1, Pallas kernels, convolve(): pl.pallas_call(convolve_kernel, out_shape=jax.ShapeDtypeStruct((8, 32, 10...  22.7 us
    pallas_call x1, Pallas kernels, deal(): pl.pallas_call(deal_kernel, in_specs=[ANY] * 2, out_specs=[ANY] * 2, out_...  14 us
    pallas_call x1, Pallas kernels, project(): pl.pallas_call(project_kernel, grid=(3,), in_specs=[pl.BlockSpec(rows.sha...  6.16 us
    unnamed x2, local copies, waits for them, and re-layouts  3.54 us

profile of v1, /device:TPU:32, one launch (start us, length us, event | category | flops | bytes accessed | tf_op | source)
XLA Modules:
  0.0 155.4 jit_solution(11520499934804908603)
XLA Ops:
  0.6 1.3 reshape.19.fine_ref
  1.9 1.2 broadcast_in_dim.7.gain_ref
  3.1 29.6 %share.1 = (bf16[16,128,256]{2,1,0:T(8,128)(2,1)}, f32[16,8,384]{2,1,0:T(8,128)}, s32[8,8,256]{2,1,0:T(8,128)}, f32[2304,256]{1,0:T(8,128)}) custom-call(s32[4,256]{1,0:T(4,128)} %reshape.19.fine_ref, s32[4,128]{1,0:T(4,128)} %bitcast.10, s32[1,256]{1,0:T(1,128)} %bitcast.11, bf16[1024,256]{1,0:T(8,128)(2,1)} %emb_fine_ref.1, ...), custom_call_target="tpu_custom_call" | custom-call | tf_op jit(solution)/shard_map/share/pallas_call | solution.py:387
  32.8 6.2 %project.1 = (bf16[3,256,256]{2,1,0:T(8,128)(2,1)}, f32[8,128]{1,0:T(8,128)}) custom-call(bf16[16,128,256]{2,1,0:T(8,128)(2,1)} %get-tuple-element.10.rows_ref, f32[16,8,384]{2,1,0:T(8,128)} %get-tuple-element.11.side_ref, bf16[3,4096,256]{2,1,0:T(8,128)(2,1)} %bitcast.6), custom_call_target="tpu_custom_call" | custom-call | tf_op jit(solution)/shard_map/project/pallas_call | solution.py:128
  38.9 14.0 %deal.1 = (bf16[16,3,32,256]{3,2,1,0:T(8,128)(2,1)}, f32[8,8,128]{2,1,0:T(8,128)}) custom-call(bf16[3,256,256]{2,1,0:T(8,128)(2,1)} %get-tuple-element.12.proj_ref, f32[8,128]{1,0:T(8,128)} %get-tuple-element.13.factor_ref), custom_call_target="tpu_custom_call" | custom-call | tf_op jit(solution)/shard_map/deal/pallas_call | solution.py:460
  52.9 0.7 dynamic-slice_convert_fusion
  53.6 0.6 reshape.23.taps_ref
  54.2 22.7 %convolve.1.y_ref = bf16[8,32,1024]{2,1,0:T(8,128)(2,1)} custom-call(bf16[16,96,256]{2,1,0:T(8,128)(2,1)} %bitcast.8, s32[8,8,256]{2,1,0:T(8,128)} %get-tuple-element.15.ids_ref, f32[64,128]{1,0:T(8,128)} %bitcast.9, f32[6,128]{1,0:T(8,128)} %reshape.23.taps_ref, f32[2304,256]{1,0:T(8,128)} %get-tuple-element.17.spec_ref, ...), custom_call_target="tpu_custom_call" | custom-call | tf_op jit(solution)/shard_map/convolve/pallas_call | solution.py:284
  76.9 75.0 %tail.1 = (bf16[256,1024]{1,0:T(8,128)(2,1)}, bf16[1024,128]{1,0:T(8,128)(2,1)}) custom-call(bf16[8,32,1024]{2,1,0:T(8,128)(2,1)} %convolve.1.y_ref, bf16[3,4096,128]{2,1,0:T(8,128)(2,1)} %bitcast.7), custom_call_target="tpu_custom_call" | custom-call | tf_op jit(solution)/shard_map/tail/pallas_call | solution.py:704
  151.9 1.9 %copy.19 = bf16[256,1024]{1,0:T(8,128)(2,1)} copy(bf16[256,1024]{1,0:T(8,128)(2,1)} %get-tuple-element.20) | data formatting | bytes 1048576
  153.8 1.7 %copy.20 = bf16[1024,128]{1,0:T(8,128)(2,1)} copy(bf16[1024,128]{1,0:T(8,128)(2,1)} %get-tuple-element.21) | data formatting | bytes 524288

commit v2 on v1

--- a/solution.py
+++ b/solution.py
@@ -71,8 +71,7 @@
     return mm(hi, table[0]) + (mm(lo, table[0]) + mm(hi, table[1]))
 
 
-def local_sums(fine_ref, coarse_ref, order_ref, emb_fine_ref, emb_coarse_ref, ids_ref, side_ref):
-    order = order_ref[...]
+def local_sums(codes_ref, order, emb_fine_ref, emb_coarse_ref, ids_ref, sums_ref):
     row = lax.broadcasted_iota(jnp.int32, (FRAME, FRAME), 0)
     pick = (row == order).astype(BF16)
     pick_half = (row[: FRAME // 2] == order // 2).astype(BF16)
@@ -82,8 +81,8 @@
         lo = (codes % 32).astype(F32).astype(BF16)
         return (mm(hi, pick) * 32.0 + mm(lo, pick)).astype(jnp.int32)
 
-    fine = looked(fine_ref[...], pick)
-    coarse = looked(coarse_ref[...], pick_half)
+    fine = looked(codes_ref[0:4, :], pick)
+    coarse = looked(codes_ref[4:8, : FRAME // 2], pick_half)
     ids_ref[0:4, :] = fine
     ids_ref[4:8, :] = coarse
     vocab = lax.broadcasted_iota(jnp.int32, (emb_fine_ref.shape[0], FRAME), 0)
@@ -97,55 +96,8 @@
         )
         rows = rows.astype(BF16).astype(F32)
         total = jnp.sum(rows * rows, axis=0, keepdims=True)
-        side_ref[2 * frame : 2 * frame + 1, FRAME:] = total[:, :LANES]
-        side_ref[2 * frame + 1 : 2 * frame + 2, FRAME:] = total[:, LANES:]
-
-
-def project_kernel(rows_ref, side_ref, w_ref, out_ref, factor_ref, x_ref):
-    chans = rows_ref.shape[0]
-
-    @pl.when(pl.program_id(0) == 0)
-    def _():
-        for c in range(chans):
-            x = rows_ref[c].astype(F32) * side_ref[c, 0:1, :FRAME]
-            hi, lo = split(x)
-            x_ref[0:128, c * 256 : (c + 1) * 256] = hi
-            x_ref[128:256, c * 256 : (c + 1) * 256] = lo
-        total = side_ref[0, :, FRAME:]
-        for c in range(1, chans):
-            total = total + side_ref[c, :, FRAME:]
-        factor_ref[...] = lax.rsqrt(total / (chans * 256.0) + EPSILON)
-
-    both = mm(x_ref[...], w_ref[0])
-    hi, lo = split(jnp.transpose(both[:128] + both[128:]))
-    out_ref[0, :, :128] = hi
-    out_ref[0, :, 128:] = lo
-
-
-def project(rows, side, w, interpret=False):
-    chans = rows.shape[0]
-    depth = w.shape[1]
-    return pl.pallas_call(
-        project_kernel,
-        grid=(3,),
-        in_specs=[
-            pl.BlockSpec(rows.shape, lambda k: (0, 0, 0)),
-            pl.BlockSpec(side.shape, lambda k: (0, 0, 0)),
-            pl.BlockSpec((1, depth, 256), lambda k: (k, 0, 0)),
-        ],
-        out_specs=[
-            pl.BlockSpec((1, 256, 256), lambda k: (k, 0, 0)),
-            pl.BlockSpec((8, LANES), lambda k: (0, 0)),
-        ],
-        out_shape=(
-            jax.ShapeDtypeStruct((3, 256, 256), BF16),
-            jax.ShapeDtypeStruct((8, LANES), F32),
-        ),
-        scratch_shapes=[pltpu.VMEM((256, chans * 256), BF16)],
-        compiler_params=pltpu.CompilerParams(vmem_limit_bytes=BIG),
-        interpret=interpret,
-        name="project",
-    )(rows, side, w)
+        sums_ref[2 * frame : 2 * frame + 1, :] = total[:, :LANES]
+        sums_ref[2 * frame + 1 : 2 * frame + 2, :] = total[:, LANES:]
 
 
 GROUP = 4
@@ -222,12 +174,15 @@
 
     tap_row = lax.broadcasted_iota(jnp.int32, (LANES, LANES), 0)
     tap_col = lax.broadcasted_iota(jnp.int32, (LANES, LANES), 1)
+    group_row = lax.broadcasted_iota(jnp.int32, taps_ref.shape[1:], 0)
     rows = 16 * TILES
     first_tile = lax.broadcasted_iota(jnp.int32, (rows, LANES), 0) % TILES == 0
     scale = jnp.concatenate([factor_ref[...]] * 16, 0)
 
     def filtered(k, g):
-        taps = jnp.broadcast_to(taps_ref[2 * k + g : 2 * k + g + 1, :], (LANES, LANES))
+        wanted = 2 * lax.axis_index("seq") + g
+        own = jnp.where(group_row == wanted, taps_ref[k].astype(F32), 0.0)
+        taps = jnp.broadcast_to(jnp.sum(own, axis=0, keepdims=True), (LANES, LANES))
         turned = pltpu.roll(taps, 0, 1, stride=1, stride_axis=0)
         both = jnp.concatenate(
             [
@@ -321,24 +276,29 @@
     return copy
 
 
-def share_kernel(
+def front_kernel(
     fine_ref,
     coarse_ref,
     order_ref,
+    gain_ref,
     emb_fine_ref,
     emb_coarse_ref,
-    gain_ref,
     filter_ref,
     outer_ref,
     twist_ref,
     fwd_ref,
-    rows_out,
-    side_out,
+    w_ref,
+    proj_out,
+    factor_out,
     ids_out,
     spec_ref,
+    codes_ref,
     rows_ref,
-    side_ref,
-    ids_ref,
+    gains_ref,
+    sums_ref,
+    x_ref,
+    wv_ref,
+    proj_ref,
     wide_ref,
     send,
     recv,
@@ -348,131 +308,125 @@
     sems = (send, recv)
     plane = [(z, lax.rem(c + j, 16), r) for j in range(1, 16)]
     line = [(lax.rem(z + j, 8), c, r) for j in range(1, 8)]
+    sibling = (z, c, 1 - r)
+    slot = r * 8 + z
+    weights = [pltpu.make_async_copy(w_ref.at[k], wv_ref.at[k], own.at[k]) for k in range(3)]
+    for copy in weights:
+        copy.start()
     at = pl.ds(pl.multiple_of(z * 128, 128), 128)
 
     @pl.when(r == 0)
     def _():
-        rows_ref[...] = emb_fine_ref[at, :]
+        rows_ref[c] = emb_fine_ref[at, :]
 
     @pl.when(r != 0)
     def _():
-        rows_ref[...] = emb_coarse_ref[at, :]
-
-    greet(plane + line)
-    copies = []
-    for j, peer in enumerate(plane):
-        copies.append(push(rows_ref, rows_out.at[c], sems, j, peer))
-    side_ref[:, :FRAME] = jnp.broadcast_to(gain_ref[...].astype(F32), (8, FRAME))
-    local_sums(fine_ref, coarse_ref, order_ref, emb_fine_ref, emb_coarse_ref, ids_ref, side_ref)
-    for j, peer in enumerate(plane):
-        copies.append(push(side_ref, side_out.at[c], sems, 15 + j, peer))
-    for j, peer in enumerate(line):
-        copies.append(push(ids_ref, ids_out.at[z], sems, 30 + j, peer))
-    mine = [
-        pltpu.make_async_copy(rows_ref, rows_out.at[c], own.at[0]),
-        pltpu.make_async_copy(side_ref, side_out.at[c], own.at[1]),
-        pltpu.make_async_copy(ids_ref, ids_out.at[z], own.at[2]),
-    ]
-    for copy in mine:
-        copy.start()
+        rows_ref[c] = emb_coarse_ref[at, :]
+
+    gains_ref[c] = jnp.broadcast_to(gain_ref[...].reshape(1, FRAME).astype(F32), (8, FRAME))
+    greet(plane + line + [sibling])
+    sent = []
+    index = [0]
+
+    def tell(src, dst, peer):
+        copy = push(src, dst, sems, index[0], peer)
+        index[0] += 1
+        sent.append(copy)
+        return copy
+
+    gains = [tell(gains_ref.at[c], gains_ref.at[c], peer) for peer in plane]
+    rows = [tell(rows_ref.at[c], rows_ref.at[c], peer) for peer in plane]
+    for i in range(4):
+        codes_ref[i : i + 1, :] = fine_ref[i * FRAME : (i + 1) * FRAME].reshape(1, FRAME)
+        codes_ref[4 + i : 5 + i, : FRAME // 2] = coarse_ref[
+            i * FRAME // 2 : (i + 1) * FRAME // 2
+        ].reshape(1, FRAME // 2)
+    local_sums(
+        codes_ref,
+        order_ref[...].reshape(1, FRAME),
+        emb_fine_ref,
+        emb_coarse_ref,
+        ids_out.at[z],
+        sums_ref.at[c],
+    )
+    sums = [tell(sums_ref.at[c], sums_ref.at[c], peer) for peer in plane]
+    ids = [tell(ids_out.at[z], ids_out.at[z], peer) for peer in line]
+
+    def prepare(origin):
+        hi, lo = split(rows_ref[origin].astype(F32) * gains_ref[origin, 0:1, :])
+        columns = pl.ds(pl.multiple_of(origin * 256, 256), 256)
+        x_ref[0:128, columns] = hi
+        x_ref[128:256, columns] = lo
+
+    prepare(c)
+    for j in range(1, 16):
+        gains[j - 1].wait_recv()
+        rows[j - 1].wait_recv()
+        prepare(lax.rem(c + 16 - j, 16))
+    dealt = [[] for _ in range(7)]
+    for k in range(3):
+        weights[k].wait()
+        both = mm(x_ref[...], wv_ref[k])
+        hi, lo = split(jnp.transpose(both[:128] + both[128:]))
+        proj_ref[k, :, :128] = hi
+        proj_ref[k, :, 128:] = lo
+        for j, peer in enumerate(line):
+            src = proj_ref.at[k, pl.ds(pl.multiple_of(peer[0] * 32, 32), 32), :]
+            dealt[j].append(tell(src, proj_out.at[slot, k], peer))
+    for copy in sums:
+        copy.wait_recv()
+    total = sums_ref[0]
+    for other in range(1, 16):
+        total = total + sums_ref[other]
+    factor_out[z] = lax.rsqrt(total / (16 * 256.0) + EPSILON)
+    factors = [tell(factor_out.at[z], factor_out.at[z], peer) for peer in line]
+    proj_out[slot] = proj_ref[:, pl.ds(pl.multiple_of(z * 32, 32), 32), :]
+    across = [tell(proj_out.at[slot], proj_out.at[slot], sibling)]
     spectrum_kernel(filter_ref, outer_ref, twist_ref, fwd_ref, spec_ref, wide_ref)
-    for copy in mine + copies:
-        copy.wait()
-
-
-def share(fine, coarse, order, emb_fine, emb_coarse, gain, long_filter):
+    for j in range(7):
+        for copy in dealt[j]:
+            copy.wait_recv()
+        landed = proj_out.at[r * 8 + lax.rem(z + 7 - j, 8)]
+        across.append(tell(landed, landed, sibling))
+    for copy in ids + factors + across:
+        copy.wait_recv()
+    for copy in sent:
+        copy.wait_send()
+
+
+def front(fine, coarse, order, gain, emb_fine, emb_coarse, long_filter, w):
     outer3, twist, fwd, _, _ = tables()
     channels = long_filter.shape[0]
     vmem = pl.BlockSpec(memory_space=pltpu.VMEM)
+    copies = 45 + 7 + 21 + 7 + 8
     return pl.pallas_call(
-        share_kernel,
-        in_specs=[vmem] * 10,
-        out_specs=[ANY, ANY, ANY, vmem],
+        front_kernel,
+        in_specs=[vmem] * 10 + [ANY],
+        out_specs=[vmem] * 4,
         out_shape=(
-            jax.ShapeDtypeStruct((16, 128, 256), BF16),
-            jax.ShapeDtypeStruct((16, 8, 384), F32),
+            jax.ShapeDtypeStruct((16, 3, 32, 256), BF16),
+            jax.ShapeDtypeStruct((8, 8, LANES), F32),
             jax.ShapeDtypeStruct((8, 8, FRAME), jnp.int32),
             jax.ShapeDtypeStruct((channels * ROWS_W, 256), F32),
         ),
         scratch_shapes=[
-            pltpu.VMEM((128, 256), BF16),
-            pltpu.VMEM((8, 384), F32),
             pltpu.VMEM((8, FRAME), jnp.int32),
+            pltpu.VMEM((16, 128, 256), BF16),
+            pltpu.VMEM((16, 8, FRAME), F32),
+            pltpu.VMEM((16, 8, LANES), F32),
+            pltpu.VMEM((256, 4096), BF16),
+            pltpu.VMEM((3, 4096, 256), BF16),
+            pltpu.VMEM((3, 256, 256), BF16),
             pltpu.VMEM((channels * TILES, LANES), F32),
-            pltpu.SemaphoreType.DMA((37,)),
-            pltpu.SemaphoreType.DMA((37,)),
+            pltpu.SemaphoreType.DMA((copies,)),
+            pltpu.SemaphoreType.DMA((copies,)),
             pltpu.SemaphoreType.DMA((3,)),
         ],
         compiler_params=pltpu.CompilerParams(
             collective_id=0, has_side_effects=True, vmem_limit_bytes=BIG
         ),
-        name="share",
-    )(
-        fine.reshape(4, FRAME),
-        coarse.reshape(4, FRAME // 2),
-        order[None],
-        emb_fine,
-        emb_coarse,
-        gain[None],
-        long_filter,
-        outer3,
-        twist,
-        fwd,
-    )
-
-
-def deal_kernel(proj_ref, factor_ref, proj_out, factor_out, send, recv, own):
-    z, c, r = here()
-    sems = (send, recv)
-    slot = r * 8 + z
-    line = [(lax.rem(z + j, 8), c, r) for j in range(1, 8)]
-    sibling = (z, c, 1 - r)
-    greet(line + [sibling])
-
-    def piece(to):
-        return proj_ref.at[:, pl.ds(pl.multiple_of(to * 32, 32), 32), :]
-
-    copies = []
-    for j, peer in enumerate(line):
-        copies.append(push(piece(peer[0]), proj_out.at[slot], sems, j, peer))
-    for j, peer in enumerate(line):
-        copies.append(push(factor_ref, factor_out.at[z], sems, 7 + j, peer))
-    across = [push(piece(z), proj_out.at[slot], sems, 14, sibling)]
-    mine = [
-        pltpu.make_async_copy(piece(z), proj_out.at[slot], own.at[0]),
-        pltpu.make_async_copy(factor_ref, factor_out.at[z], own.at[1]),
-    ]
-    for copy in mine:
-        copy.start()
-    for j in range(7):
-        copies[j].wait_recv()
-        landed = proj_out.at[r * 8 + lax.rem(z + 7 - j, 8)]
-        across.append(push(landed, landed, sems, 15 + j, sibling))
-    for copy in across + copies[7:]:
-        copy.wait_recv()
-    for copy in across + copies:
-        copy.wait_send()
-    for copy in mine:
-        copy.wait()
-
-
-def deal(proj, factor):
-    return pl.pallas_call(
-        deal_kernel,
-        in_specs=[ANY] * 2,
-        out_specs=[ANY] * 2,
-        out_shape=(
-            jax.ShapeDtypeStruct((16, 3, 32, 256), BF16),
-            jax.ShapeDtypeStruct((8, 8, LANES), F32),
-        ),
-        scratch_shapes=[
-            pltpu.SemaphoreType.DMA((22,)),
-            pltpu.SemaphoreType.DMA((22,)),
-            pltpu.SemaphoreType.DMA((2,)),
-        ],
-        compiler_params=pltpu.CompilerParams(collective_id=1, has_side_effects=True),
-        name="deal",
-    )(proj, factor)
+        name="front",
+    )(fine, coarse, order, gain, emb_fine, emb_coarse, long_filter, outer3, twist, fwd, w)
 
 
 CHUNKS = 2
@@ -741,15 +695,18 @@
     long_filter,
     w_attn,
 ):
-    z = lax.axis_index("seq")
-    rows_all, side_all, ids_all, spec = share(
-        fine_codes, coarse_codes, frame_order, emb_fine, emb_coarse, norm_gain, long_filter
+    proj_all, factor_all, ids_all, spec = front(
+        fine_codes,
+        coarse_codes,
+        frame_order,
+        norm_gain,
+        emb_fine,
+        emb_coarse,
+        long_filter,
+        jnp.transpose(w_hyena, (1, 0, 2)),
     )
-    proj, factor = project(rows_all, side_all, jnp.transpose(w_hyena, (1, 0, 2)))
-    proj_all, factor_all = deal(proj, factor)
-    taps = lax.dynamic_slice_in_dim(short_taps, z * 2, 2, 1).reshape(6, LANES).astype(F32)
     y = convolve(
-        proj_all.reshape(16, 96, 256), ids_all, factor_all.reshape(TILES, LANES), taps, spec
+        proj_all.reshape(16, 96, 256), ids_all, factor_all.reshape(TILES, LANES), short_taps, spec
     )
     return tail(y, jnp.transpose(w_attn, (1, 0, 2)))
 

time: 156 us -> 144 us (0.923)
  Pallas kernels: 147 us -> 139 us
  local copies, waits for them, and re-layouts: 6.65 us -> 3.54 us
    pallas_call x3 -> x1, Pallas kernels: 49.7 us -> 42 us  [front(): pl.pallas_call(front_kernel, in_specs=[vmem] * 10 + [ANY], out_specs=[vme...]
where the time goes in v2:
time: 144 us; the launch traced here: 143 us
  Pallas kernels  139 us (97%)
  local copies, waits for them, and re-layouts  3.54 us (2%)
    pallas_call x1, Pallas kernels, tail(): pl.pallas_call(tail_kernel, in_specs=[ANY, ANY], out_specs=[ANY, vmem], o...  74.3 us
    pallas_call x1, Pallas kernels, front(): pl.pallas_call(front_kernel, in_specs=[vmem] * 10 + [ANY], out_specs=[vme...  42 us
    pallas_call x1, Pallas kernels, convolve(): pl.pallas_call(convolve_kernel, out_shape=jax.ShapeDtypeStruct((8, 32, 10...  22.6 us
    unnamed x2, local copies, waits for them, and re-layouts  3.54 us

profile of v2, /device:TPU:32, one launch (start us, length us, event | category | flops | bytes accessed | tf_op | source)
XLA Modules:
  0.0 143.1 jit_solution(2679634749367927660)
XLA Ops:
  0.6 42.0 %front.1 = (bf16[16,3,32,256]{3,2,1,0:T(8,128)(2,1)}, f32[8,8,128]{2,1,0:T(8,128)}, s32[8,8,256]{2,1,0:T(8,128)}, f32[2304,256]{1,0:T(8,128)}) custom-call(s32[1024]{0:T(1024)} %fine_ref.1, s32[512]{0:T(512)} %coarse_ref.1, s32[256]{0:T(256)} %order_ref.1, bf16[256]{0:T(256)(128)(2,1)} %gain_ref.1, bf16[1024,256]{1,0:T(8,128)(2,1)} %emb_fine_ref.1, ...), custom_call_target="tpu_custom_call" | custom-call | tf_op jit(solution)/shard_map/front/pallas_call | solution.py:402
  42.7 22.6 %convolve.1.y_ref = bf16[8,32,1024]{2,1,0:T(8,128)(2,1)} custom-call(bf16[16,96,256]{2,1,0:T(8,128)(2,1)} %bitcast.6, s32[8,8,256]{2,1,0:T(8,128)} %get-tuple-element.7.ids_ref, f32[64,128]{1,0:T(8,128)} %bitcast.7, bf16[3,16,128]{2,1,0:T(8,128)(2,1)} %taps_ref.1, f32[2304,256]{1,0:T(8,128)} %get-tuple-element.9.spec_ref, ...), custom_call_target="tpu_custom_call" | custom-call | tf_op jit(solution)/shard_map/convolve/pallas_call | solution.py:239
  65.3 74.3 %tail.1 = (bf16[256,1024]{1,0:T(8,128)(2,1)}, bf16[1024,128]{1,0:T(8,128)(2,1)}) custom-call(bf16[8,32,1024]{2,1,0:T(8,128)(2,1)} %convolve.1.y_ref, bf16[3,4096,128]{2,1,0:T(8,128)(2,1)} %bitcast.5), custom_call_target="tpu_custom_call" | custom-call | tf_op jit(solution)/shard_map/tail/pallas_call | solution.py:658
  139.6 1.9 %copy.19 = bf16[256,1024]{1,0:T(8,128)(2,1)} copy(bf16[256,1024]{1,0:T(8,128)(2,1)} %get-tuple-element.12) | data formatting | bytes 1048576
  141.4 1.7 %copy.20 = bf16[1024,128]{1,0:T(8,128)(2,1)} copy(bf16[1024,128]{1,0:T(8,128)(2,1)} %get-tuple-element.13) | data formatting | bytes 524288

commit v3 on v2

--- a/solution.py
+++ b/solution.py
@@ -100,7 +100,7 @@
         sums_ref[2 * frame + 1 : 2 * frame + 2, :] = total[:, LANES:]
 
 
-GROUP = 4
+GROUP = 16
 
 
 def twisted(step, twist_ref):
@@ -483,7 +483,8 @@
             pltpu.make_async_copy(y_ref.at[z, :, at], x_ref.at[mine_rows, at], own.at[1 + t])
         )
         kept[-1].start()
-        turned.append([tell(y_ref.at[p[0], :, at], x_ref.at[mine_rows, at], p) for p in line])
+        if t == 0:
+            turned.append([tell(y_ref.at[p[0], :, at], x_ref.at[mine_rows, at], p) for p in line])
     half = x_ref.shape[0] // 2
     quarter = half // 2
 
@@ -541,6 +542,9 @@
         kept[t].wait()
         for copy in turned[t]:
             copy.wait_recv()
+        if t + 1 < CHUNKS:
+            at = pl.ds((t + 1) * span, span)
+            turned.append([tell(y_ref.at[p[0], :, at], x_ref.at[mine_rows, at], p) for p in line])
         for lead in range(2):
             for d in (1, -1):
                 first[t, lead, d] = send_block(t, lead, 0, 0, None, d, 0)
@@ -559,11 +563,8 @@
         for e in (1, -1):
             pending.append((t, lead, along, e))
 
-    for t in range(CHUNKS):
-        open_chunk(t)
+    open_chunk(0)
     weights.wait()
-    back = pltpu.make_async_copy(x_ref, hyena_ref, own.at[CHUNKS + 1])
-    back.start()
     for t in range(CHUNKS):
         for d in (1, -1):
             for lead in range(2):
@@ -572,6 +573,11 @@
                 for e in (1, -1):
                     second[t, lead, d, e] = send_block(t, lead, d, 0, None, e, 1)
                 pending.append((t, lead, d, 0))
+        if t + 1 < CHUNKS:
+            open_chunk(t + 1)
+        else:
+            back = pltpu.make_async_copy(x_ref, hyena_ref, own.at[CHUNKS + 1])
+            back.start()
         drain(2)
         for lead in range(2):
             onward(t, lead, 0)
@@ -683,6 +689,22 @@
     )(y, w)
 
 
+def settle_kernel(hyena_ref, attn_ref, hyena_out, attn_out):
+    hyena_out[...] = hyena_ref[...]
+    attn_out[...] = attn_ref[...]
+
+
+def settle(hyena, attn):
+    return pl.pallas_call(
+        settle_kernel,
+        out_shape=(
+            jax.ShapeDtypeStruct(hyena.shape, hyena.dtype),
+            jax.ShapeDtypeStruct(attn.shape, attn.dtype),
+        ),
+        name="settle",
+    )(hyena, attn)
+
+
 def shards(
     fine_codes,
     coarse_codes,
@@ -708,7 +730,7 @@
     y = convolve(
         proj_all.reshape(16, 96, 256), ids_all, factor_all.reshape(TILES, LANES), short_taps, spec
     )
-    return tail(y, jnp.transpose(w_attn, (1, 0, 2)))
+    return settle(*tail(y, jnp.transpose(w_attn, (1, 0, 2))))
 
 
 def solution(mesh):

time: 144 us -> 139 us (0.965)
  local copies, waits for them, and re-layouts: 3.54 us -> 0 us
  Pallas kernels: 139 us -> 137 us
    unnamed x2 -> x0, local copies, waits for them, and re-layouts: 3.54 us -> none
    pallas_call x1, Pallas kernels: 22.6 us -> 19.3 us  [convolve(): pl.pallas_call(convolve_kernel, out_shape=jax.ShapeDtypeStruct((8, 32, 10...]
    pallas_call x0 -> x1, Pallas kernels: none -> 2.02 us  [settle(): pl.pallas_call(settle_kernel, out_shape=(jax.ShapeDtypeStruct(hyena.shape...]
where the time goes in v3:
time: 139 us; the launch traced here: 138 us
  Pallas kernels  137 us (99%)
    pallas_call x1, Pallas kernels, tail(): pl.pallas_call(tail_kernel, in_specs=[ANY, ANY], out_specs=[ANY, vmem], o...  73.8 us
    pallas_call x1, Pallas kernels, front(): pl.pallas_call(front_kernel, in_specs=[vmem] * 10 + [ANY], out_specs=[vme...  42 us
    pallas_call x1, Pallas kernels, convolve(): pl.pallas_call(convolve_kernel, out_shape=jax.ShapeDtypeStruct((8, 32, 10...  19.3 us

profile of v3, /device:TPU:32, one launch (start us, length us, event | category | flops | bytes accessed | tf_op | source)
XLA Modules:
  0.0 137.8 jit_solution(18142186197519666459)
XLA Ops:
  0.6 42.0 %front.1 = (bf16[16,3,32,256]{3,2,1,0:T(8,128)(2,1)}, f32[8,8,128]{2,1,0:T(8,128)}, s32[8,8,256]{2,1,0:T(8,128)}, f32[2304,256]{1,0:T(8,128)}) custom-call(s32[1024]{0:T(1024)} %fine_ref.1, s32[512]{0:T(512)} %coarse_ref.1, s32[256]{0:T(256)} %order_ref.1, bf16[256]{0:T(256)(128)(2,1)} %gain_ref.1, bf16[1024,256]{1,0:T(8,128)(2,1)} %emb_fine_ref.1, ...), custom_call_target="tpu_custom_call" | custom-call | tf_op jit(solution)/shard_map/front/pallas_call | solution.py:402
  42.7 19.3 %convolve.1.y_ref = bf16[8,32,1024]{2,1,0:T(8,128)(2,1)} custom-call(bf16[16,96,256]{2,1,0:T(8,128)(2,1)} %bitcast.6, s32[8,8,256]{2,1,0:T(8,128)} %get-tuple-element.9.ids_ref, f32[64,128]{1,0:T(8,128)} %bitcast.7, bf16[3,16,128]{2,1,0:T(8,128)(2,1)} %taps_ref.1, f32[2304,256]{1,0:T(8,128)} %get-tuple-element.11.spec_ref, ...), custom_call_target="tpu_custom_call" | custom-call | tf_op jit(solution)/shard_map/convolve/pallas_call | solution.py:239
  62.0 73.8 %tail.1 = (bf16[256,1024]{1,0:T(8,128)(2,1)}, bf16[1024,128]{1,0:T(8,128)(2,1)}) custom-call(bf16[8,32,1024]{2,1,0:T(8,128)(2,1)} %convolve.1.y_ref, bf16[3,4096,128]{2,1,0:T(8,128)(2,1)} %bitcast.5), custom_call_target="tpu_custom_call" | custom-call | tf_op jit(solution)/shard_map/tail/pallas_call | solution.py:664
  135.8 2.0 %settle.1 = (bf16[256,1024]{1,0:T(8,128)(2,1)}, bf16[1024,128]{1,0:T(8,128)(2,1)}) custom-call(bf16[256,1024]{1,0:T(8,128)(2,1)} %get-tuple-element.12.hyena_ref, bf16[1024,128]{1,0:T(8,128)(2,1)} %get-tuple-element.13.attn_ref), custom_call_target="tpu_custom_call" | custom-call | tf_op jit(solution)/shard_map/settle/pallas_call | solution.py:698

commit v4 on v3

--- a/solution.py
+++ b/solution.py
@@ -335,7 +335,60 @@
         return copy
 
     gains = [tell(gains_ref.at[c], gains_ref.at[c], peer) for peer in plane]
-    rows = [tell(rows_ref.at[c], rows_ref.at[c], peer) for peer in plane]
+    y, x = c // 4, lax.rem(c, 4)
+
+    def chan(at_x, at_y):
+        return lax.rem(at_y + 8, 4) * 4 + lax.rem(at_x + 8, 4)
+
+    def hop(lead, along, across, part, direction, phase):
+        axes = (0, 1) if lead == 0 else (1, 0)
+        offset = [0, 0]
+        offset[axes[0]], offset[axes[1]] = along, across
+        step = [0, 0]
+        step[axes[phase]] = direction
+        target = (z, chan(x + step[0], y + step[1]), r)
+        part_rows = pl.ds(lead * 64 + (0 if part is None else part * 32), 64 if part is None else 32)
+        block = rows_ref.at[chan(x - offset[0], y - offset[1]), part_rows]
+        number = index[0]
+        tell(block, block, target)
+        landed = rows_ref.at[chan(x - offset[0] - step[0], y - offset[1] - step[1]), part_rows]
+        return pltpu.make_async_remote_copy(
+            src_ref=landed,
+            dst_ref=landed,
+            send_sem=send.at[number],
+            recv_sem=recv.at[number],
+            device_id=target,
+            device_id_type=MESH,
+        )
+
+    first = {(lead, d): hop(lead, 0, 0, None, d, 0) for lead in range(2) for d in (1, -1)}
+    second = {(lead, 0, d): hop(lead, 0, 0, None, d, 1) for lead in range(2) for d in (1, -1)}
+    turned = {}
+    for d in (1, -1):
+        for lead in range(2):
+            first[lead, d].wait_recv()
+            turned[lead, d] = hop(lead, d, 0, 0 if d == 1 else 1, d, 0)
+            for e in (1, -1):
+                second[lead, d, e] = hop(lead, d, 0, None, e, 1)
+    last = []
+
+    def onward(lead, along):
+        for e in (1, -1):
+            second[lead, along, e].wait_recv()
+            last.append(hop(lead, along, e, 0 if e == 1 else 1, e, 1))
+
+    for lead in range(2):
+        onward(lead, 0)
+    for lead in range(2):
+        turned[lead, 1].wait_recv()
+        turned[lead, -1].wait_recv()
+        for e in (1, -1):
+            second[lead, 2, e] = hop(lead, 2, 0, None, e, 1)
+    for along in (1, -1):
+        for lead in range(2):
+            onward(lead, along)
+    for lead in range(2):
+        onward(lead, 2)
     for i in range(4):
         codes_ref[i : i + 1, :] = fine_ref[i * FRAME : (i + 1) * FRAME].reshape(1, FRAME)
         codes_ref[4 + i : 5 + i, : FRAME // 2] = coarse_ref[
@@ -358,11 +411,13 @@
         x_ref[0:128, columns] = hi
         x_ref[128:256, columns] = lo
 
+    for arrival in last:
+        arrival.wait_recv()
+    for copy in gains:
+        copy.wait_recv()
     prepare(c)
-    for j in range(1, 16):
-        gains[j - 1].wait_recv()
-        rows[j - 1].wait_recv()
-        prepare(lax.rem(c + 16 - j, 16))
+    for other in range(1, 16):
+        prepare(lax.rem(c + other, 16))
     dealt = [[] for _ in range(7)]
     for k in range(3):
         weights[k].wait()
@@ -398,7 +453,7 @@
     outer3, twist, fwd, _, _ = tables()
     channels = long_filter.shape[0]
     vmem = pl.BlockSpec(memory_space=pltpu.VMEM)
-    copies = 45 + 7 + 21 + 7 + 8
+    copies = 30 + 40 + 7 + 21 + 7 + 8
     return pl.pallas_call(
         front_kernel,
         in_specs=[vmem] * 10 + [ANY],

time: 139 us -> 136 us (0.978)
    pallas_call x1, Pallas kernels: 42 us -> 40.6 us  [front(): pl.pallas_call(front_kernel, in_specs=[vmem] * 10 + [ANY], out_specs=[vme...]
where the time goes in v4:
time: 136 us
  Pallas kernels  136 us (100%)
    pallas_call x1, Pallas kernels, tail(): pl.pallas_call(tail_kernel, in_specs=[ANY, ANY], out_specs=[ANY, vmem], o...  73.6 us
    pallas_call x1, Pallas kernels, front(): pl.pallas_call(front_kernel, in_specs=[vmem] * 10 + [ANY], out_specs=[vme...  40.6 us
    pallas_call x1, Pallas kernels, convolve(): pl.pallas_call(convolve_kernel, out_shape=jax.ShapeDtypeStruct((8, 32, 10...  19.3 us

profile of v4, /device:TPU:32, one launch (start us, length us, event | category | flops | bytes accessed | tf_op | source)
XLA Modules:
  0.0 136.2 jit_solution(15837660483976652885)
XLA Ops:
  0.6 40.6 %front.1 = (bf16[16,3,32,256]{3,2,1,0:T(8,128)(2,1)}, f32[8,8,128]{2,1,0:T(8,128)}, s32[8,8,256]{2,1,0:T(8,128)}, f32[2304,256]{1,0:T(8,128)}) custom-call(s32[1024]{0:T(1024)} %fine_ref.1, s32[512]{0:T(512)} %coarse_ref.1, s32[256]{0:T(256)} %order_ref.1, bf16[256]{0:T(256)(128)(2,1)} %gain_ref.1, bf16[1024,256]{1,0:T(8,128)(2,1)} %emb_fine_ref.1, ...), custom_call_target="tpu_custom_call" | custom-call | tf_op jit(solution)/shard_map/front/pallas_call | solution.py:457
  41.2 19.3 %convolve.1.y_ref = bf16[8,32,1024]{2,1,0:T(8,128)(2,1)} custom-call(bf16[16,96,256]{2,1,0:T(8,128)(2,1)} %bitcast.6, s32[8,8,256]{2,1,0:T(8,128)} %get-tuple-element.9.ids_ref, f32[64,128]{1,0:T(8,128)} %bitcast.7, bf16[3,16,128]{2,1,0:T(8,128)(2,1)} %taps_ref.1, f32[2304,256]{1,0:T(8,128)} %get-tuple-element.11.spec_ref, ...), custom_call_target="tpu_custom_call" | custom-call | tf_op jit(solution)/shard_map/convolve/pallas_call | solution.py:239
  60.5 73.6 %tail.1 = (bf16[256,1024]{1,0:T(8,128)(2,1)}, bf16[1024,128]{1,0:T(8,128)(2,1)}) custom-call(bf16[8,32,1024]{2,1,0:T(8,128)(2,1)} %convolve.1.y_ref, bf16[3,4096,128]{2,1,0:T(8,128)(2,1)} %bitcast.5), custom_call_target="tpu_custom_call" | custom-call | tf_op jit(solution)/shard_map/tail/pallas_call | solution.py:719
  134.1 2.0 %settle.1 = (bf16[256,1024]{1,0:T(8,128)(2,1)}, bf16[1024,128]{1,0:T(8,128)(2,1)}) custom-call(bf16[256,1024]{1,0:T(8,128)(2,1)} %get-tuple-element.12.hyena_ref, bf16[1024,128]{1,0:T(8,128)(2,1)} %get-tuple-element.13.attn_ref), custom_call_target="tpu_custom_call" | custom-call | tf_op jit(solution)/shard_map/settle/pallas_call | solution.py:753

commit v5 on v4

--- a/solution.py
+++ b/solution.py
@@ -150,8 +150,9 @@
 ):
     channels = 32
     for s in range(16):
-        left_ref[0:96, s * 128 : (s + 1) * 128] = proj_ref[s, :, :128]
-        left_ref[96:192, s * 128 : (s + 1) * 128] = proj_ref[s, :, 128:]
+        both = proj_ref[s].reshape(96, 256)
+        left_ref[0:96, s * 128 : (s + 1) * 128] = both[:, :128]
+        left_ref[96:192, s * 128 : (s + 1) * 128] = both[:, 128:]
     vocab = lax.broadcasted_iota(jnp.int32, (1024, FRAME), 0)
 
     @pl.loop(0, 8)
@@ -177,7 +178,7 @@
     group_row = lax.broadcasted_iota(jnp.int32, taps_ref.shape[1:], 0)
     rows = 16 * TILES
     first_tile = lax.broadcasted_iota(jnp.int32, (rows, LANES), 0) % TILES == 0
-    scale = jnp.concatenate([factor_ref[...]] * 16, 0)
+    scale = jnp.concatenate([factor_ref[...].reshape(TILES, LANES)] * 16, 0)
 
     def filtered(k, g):
         wanted = 2 * lax.axis_index("seq") + g
@@ -234,24 +235,6 @@
         ].astype(BF16)
 
 
-def convolve(proj, ids, factor, taps, spec, interpret=False):
-    outer3, twist, fwd, bwd, inv3 = tables()
-    return pl.pallas_call(
-        convolve_kernel,
-        out_shape=jax.ShapeDtypeStruct((8, 32, 1024), BF16),
-        scratch_shapes=[
-            pltpu.VMEM((192, 2048), BF16),
-            pltpu.VMEM((96 * TILES, LANES), F32),
-            pltpu.VMEM((32 * TILES, LANES), BF16),
-            pltpu.VMEM((32 * TILES, LANES), BF16),
-            pltpu.VMEM((32 * TILES, LANES), F32),
-        ],
-        compiler_params=pltpu.CompilerParams(vmem_limit_bytes=BIG),
-        interpret=interpret,
-        name="convolve",
-    )(proj, ids, factor, taps, spec, outer3, twist, fwd, bwd, inv3)
-
-
 def here():
     return lax.axis_index("seq"), lax.axis_index("chan"), lax.axis_index("rep")
 
@@ -287,11 +270,20 @@
     outer_ref,
     twist_ref,
     fwd_ref,
+    bwd_ref,
+    inv_ref,
+    taps_ref,
     w_ref,
+    out_ref,
     proj_out,
     factor_out,
     ids_out,
     spec_ref,
+    left_ref,
+    all_ref,
+    gate_ref,
+    mix_ref,
+    y_ref,
     codes_ref,
     rows_ref,
     gains_ref,
@@ -445,26 +437,47 @@
         across.append(tell(landed, landed, sibling))
     for copy in ids + factors + across:
         copy.wait_recv()
+    convolve_kernel(
+        proj_out,
+        ids_out,
+        factor_out,
+        taps_ref,
+        spec_ref,
+        outer_ref,
+        twist_ref,
+        fwd_ref,
+        bwd_ref,
+        inv_ref,
+        out_ref,
+        left_ref,
+        all_ref,
+        gate_ref,
+        mix_ref,
+        y_ref,
+    )
     for copy in sent:
         copy.wait_send()
 
 
-def front(fine, coarse, order, gain, emb_fine, emb_coarse, long_filter, w):
-    outer3, twist, fwd, _, _ = tables()
+def front(fine, coarse, order, gain, emb_fine, emb_coarse, long_filter, taps, w):
+    outer3, twist, fwd, bwd, inv3 = tables()
     channels = long_filter.shape[0]
     vmem = pl.BlockSpec(memory_space=pltpu.VMEM)
     copies = 30 + 40 + 7 + 21 + 7 + 8
     return pl.pallas_call(
         front_kernel,
-        in_specs=[vmem] * 10 + [ANY],
-        out_specs=[vmem] * 4,
-        out_shape=(
-            jax.ShapeDtypeStruct((16, 3, 32, 256), BF16),
-            jax.ShapeDtypeStruct((8, 8, LANES), F32),
-            jax.ShapeDtypeStruct((8, 8, FRAME), jnp.int32),
-            jax.ShapeDtypeStruct((channels * ROWS_W, 256), F32),
-        ),
+        in_specs=[vmem] * 13 + [ANY],
+        out_shape=jax.ShapeDtypeStruct((8, channels, 1024), BF16),
         scratch_shapes=[
+            pltpu.VMEM((16, 3, 32, 256), BF16),
+            pltpu.VMEM((8, 8, LANES), F32),
+            pltpu.VMEM((8, 8, FRAME), jnp.int32),
+            pltpu.VMEM((channels * ROWS_W, 256), F32),
+            pltpu.VMEM((192, 2048), BF16),
+            pltpu.VMEM((96 * TILES, LANES), F32),
+            pltpu.VMEM((channels * TILES, LANES), BF16),
+            pltpu.VMEM((channels * TILES, LANES), BF16),
+            pltpu.VMEM((channels * TILES, LANES), F32),
             pltpu.VMEM((8, FRAME), jnp.int32),
             pltpu.VMEM((16, 128, 256), BF16),
             pltpu.VMEM((16, 8, FRAME), F32),
@@ -481,7 +494,7 @@
             collective_id=0, has_side_effects=True, vmem_limit_bytes=BIG
         ),
         name="front",
-    )(fine, coarse, order, gain, emb_fine, emb_coarse, long_filter, outer3, twist, fwd, w)
+    )(fine, coarse, order, gain, emb_fine, emb_coarse, long_filter, outer3, twist, fwd, bwd, inv3, taps, w)
 
 
 CHUNKS = 2
@@ -772,7 +785,7 @@
     long_filter,
     w_attn,
 ):
-    proj_all, factor_all, ids_all, spec = front(
+    y = front(
         fine_codes,
         coarse_codes,
         frame_order,
@@ -780,10 +793,8 @@
         emb_fine,
         emb_coarse,
         long_filter,
+        short_taps,
         jnp.transpose(w_hyena, (1, 0, 2)),
-    )
-    y = convolve(
-        proj_all.reshape(16, 96, 256), ids_all, factor_all.reshape(TILES, LANES), short_taps, spec
     )
     return settle(*tail(y, jnp.transpose(w_attn, (1, 0, 2))))
 

time: 136 us -> 133 us (0.978)
  Pallas kernels: 136 us -> 132 us
    pallas_call x2 -> x1, Pallas kernels: 59.9 us -> 55.9 us  [front(): pl.pallas_call(front_kernel, in_specs=[vmem] * 13 + [ANY], out_shape=jax....]
where the time goes in v5:
time: 133 us
  Pallas kernels  132 us (99%)
    pallas_call x1, Pallas kernels, tail(): pl.pallas_call(tail_kernel, in_specs=[ANY, ANY], out_specs=[ANY, vmem], o...  74.1 us
    pallas_call x1, Pallas kernels, front(): pl.pallas_call(front_kernel, in_specs=[vmem] * 13 + [ANY], out_shape=jax....  55.9 us

profile of v5, /device:TPU:32, one launch (start us, length us, event | category | flops | bytes accessed | tf_op | source)
XLA Modules:
  0.0 132.7 jit_solution(17788743818835179308)
XLA Ops:
  0.6 55.9 %front.1.y_ref = bf16[8,32,1024]{2,1,0:T(8,128)(2,1)} custom-call(s32[1024]{0:T(1024)} %fine_ref.1, s32[512]{0:T(512)} %coarse_ref.1, s32[256]{0:T(256)} %order_ref.1, bf16[256]{0:T(256)(128)(2,1)} %gain_ref.1, bf16[1024,256]{1,0:T(8,128)(2,1)} %emb_fine_ref.1, bf16[1024,256]{1,0:T(8,128)(2,1)} %emb_coarse_ref.1, f32[32,8192]{1,0:T(8,128)} %filter_ref.1, ...), custom_call_target="tpu_custom_call" | custom-call | tf_op jit(solution)/shard_map/front/pallas_call | solution.py:467
  56.6 74.1 %tail.1 = (bf16[256,1024]{1,0:T(8,128)(2,1)}, bf16[1024,128]{1,0:T(8,128)(2,1)}) custom-call(bf16[8,32,1024]{2,1,0:T(8,128)(2,1)} %front.1.y_ref, bf16[3,4096,128]{2,1,0:T(8,128)(2,1)} %bitcast.3), custom_call_target="tpu_custom_call" | custom-call | tf_op jit(solution)/shard_map/tail/pallas_call | solution.py:732
  130.7 2.0 %settle.1 = (bf16[256,1024]{1,0:T(8,128)(2,1)}, bf16[1024,128]{1,0:T(8,128)(2,1)}) custom-call(bf16[256,1024]{1,0:T(8,128)(2,1)} %get-tuple-element.4.hyena_ref, bf16[1024,128]{1,0:T(8,128)(2,1)} %get-tuple-element.5.attn_ref), custom_call_target="tpu_custom_call" | custom-call | tf_op jit(solution)/shard_map/settle/pallas_call | solution.py:766

commit v6 on v5

--- a/solution.py
+++ b/solution.py
@@ -529,9 +529,15 @@
     def device(at_x, at_y):
         return (z, chan(at_x, at_y), r)
 
-    line = [(lax.rem(z + j, 8), c, r) for j in range(1, 8)]
-    weights = pltpu.make_async_copy(w_ref, wv_ref, own.at[0])
-    weights.start()
+    line = [(lax.rem(z + j, 8), c, r) for j in (4, 3, 5, 2, 6, 1, 7)]
+    weights = [
+        pltpu.make_async_copy(
+            w_ref.at[k], wv_ref.at[:, pl.ds(k * HD, HD)], own.at[CHUNKS + 2 + k]
+        )
+        for k in range(3)
+    ]
+    for copy in weights:
+        copy.start()
     greet(line + [device(x + 1, y), device(x - 1, y), device(x, y + 1), device(x, y - 1)])
     index = [0]
     sent = []
@@ -593,14 +599,13 @@
         origin = chan(x - offset[0], y - offset[1])
         block = x_ref[rows, at] if offset == (0, 0) else land_ref[origin, rows, at]
         depth = pl.ds(pl.multiple_of(origin * 2 * half + lead * half, half), half)
-        for k in range(3):
-            product = lax.dot_general(
-                wv_ref[k, depth, :], block, (((0,), (0,)), ((), ())), preferred_element_type=F32
-            )
-            if (along, across, lead) == (0, 0, 0):
-                acc_ref[k, :, at] = product
-            else:
-                acc_ref[k, :, at] += product
+        product = lax.dot_general(
+            wv_ref[depth, :], block, (((0,), (0,)), ((), ())), preferred_element_type=F32
+        )
+        if (along, across, lead) == (0, 0, 0):
+            acc_ref[:, at] = product
+        else:
+            acc_ref[:, at] += product
 
     def drain(count):
         for _ in range(min(count, len(pending))):
@@ -632,7 +637,8 @@
             pending.append((t, lead, along, e))
 
     open_chunk(0)
-    weights.wait()
+    for copy in weights:
+        copy.wait()
     for t in range(CHUNKS):
         for d in (1, -1):
             for lead in range(2):
@@ -661,7 +667,7 @@
         for along in (1, -1, 2):
             for lead in range(2):
                 onward(t, lead, along)
-                drain(3)
+                drain(5)
     for t, lead, along, arrival in last:
         arrival.wait_recv()
     for position in range(0, len(last), 2):
@@ -670,7 +676,7 @@
     drain(len(pending))
 
     blocks = length // BLOCK
-    heads = [[acc_ref[k, :, b * BLOCK : (b + 1) * BLOCK].astype(BF16) for b in range(blocks)] for k in range(3)]
+    heads = [[acc_ref[k * HD : (k + 1) * HD, b * BLOCK : (b + 1) * BLOCK].astype(BF16) for b in range(blocks)] for k in range(3)]
     states = [
         lax.dot_general(
             heads[1][b], heads[2][b], (((1,), (1,)), ((), ())), preferred_element_type=F32
@@ -738,17 +744,17 @@
             jax.ShapeDtypeStruct((length, HD), BF16),
         ),
         scratch_shapes=[
-            pltpu.VMEM(w.shape, BF16),
+            pltpu.VMEM((w.shape[1], 3 * HD), BF16),
             pltpu.VMEM((depth, length), BF16),
             pltpu.VMEM((16, depth, length), BF16),
-            pltpu.VMEM((3, HD, length), F32),
+            pltpu.VMEM((3 * HD, length), F32),
             pltpu.VMEM((8, HD // 8, HD), F32),
             pltpu.VMEM((8, HD // 8, HD), F32),
             pltpu.VMEM((8, HD // 8, HD), F32),
             pltpu.VMEM((8, HD // 8, HD), F32),
             pltpu.SemaphoreType.DMA((copies,)),
             pltpu.SemaphoreType.DMA((copies,)),
-            pltpu.SemaphoreType.DMA((CHUNKS + 2,)),
+            pltpu.SemaphoreType.DMA((CHUNKS + 5,)),
         ],
         compiler_params=pltpu.CompilerParams(
             collective_id=2, has_side_effects=True, vmem_limit_bytes=BIG

time: 133 us -> 131 us (0.985)
  Pallas kernels: 132 us -> 130 us
    pallas_call x1, Pallas kernels: 74.1 us -> 72 us  [tail(): pl.pallas_call(tail_kernel, in_specs=[ANY, ANY], out_specs=[ANY, vmem], o...]
where the time goes in v6:
time: 131 us; the launch traced here: 130 us
  Pallas kernels  130 us (99%)
    pallas_call x1, Pallas kernels, tail(): pl.pallas_call(tail_kernel, in_specs=[ANY, ANY], out_specs=[ANY, vmem], o...  72 us
    pallas_call x1, Pallas kernels, front(): pl.pallas_call(front_kernel, in_specs=[vmem] * 13 + [ANY], out_shape=jax....  55.8 us

profile of v6, /device:TPU:32, one launch (start us, length us, event | category | flops | bytes accessed | tf_op | source)
XLA Modules:
  0.0 130.5 jit_solution(1882856557354216978)
XLA Ops:
  0.6 55.8 %front.1.y_ref = bf16[8,32,1024]{2,1,0:T(8,128)(2,1)} custom-call(s32[1024]{0:T(1024)} %fine_ref.1, s32[512]{0:T(512)} %coarse_ref.1, s32[256]{0:T(256)} %order_ref.1, bf16[256]{0:T(256)(128)(2,1)} %gain_ref.1, bf16[1024,256]{1,0:T(8,128)(2,1)} %emb_fine_ref.1, bf16[1024,256]{1,0:T(8,128)(2,1)} %emb_coarse_ref.1, f32[32,8192]{1,0:T(8,128)} %filter_ref.1, ...), custom_call_target="tpu_custom_call" | custom-call | tf_op jit(solution)/shard_map/front/pallas_call | solution.py:467
  56.4 72.0 %tail.1 = (bf16[256,1024]{1,0:T(8,128)(2,1)}, bf16[1024,128]{1,0:T(8,128)(2,1)}) custom-call(bf16[8,32,1024]{2,1,0:T(8,128)(2,1)} %front.1.y_ref, bf16[3,4096,128]{2,1,0:T(8,128)(2,1)} %bitcast.3), custom_call_target="tpu_custom_call" | custom-call | tf_op jit(solution)/shard_map/tail/pallas_call | solution.py:738
  128.4 2.0 %settle.1 = (bf16[256,1024]{1,0:T(8,128)(2,1)}, bf16[1024,128]{1,0:T(8,128)(2,1)}) custom-call(bf16[256,1024]{1,0:T(8,128)(2,1)} %get-tuple-element.4.hyena_ref, bf16[1024,128]{1,0:T(8,128)(2,1)} %get-tuple-element.5.attn_ref), custom_call_target="tpu_custom_call" | custom-call | tf_op jit(solution)/shard_map/settle/pallas_call | solution.py:772
